TPU v7x, 32 devices: a whole 2x2x4 slice. The times are simulated.
32 devices in a mesh: lon: 8 (over z, y), lat: 4 (over x, core).
Axes of the slice: x: 2, y: 2, z: 4, core: 2. Of those that a mesh axis runs over, the one named last changes fastest.
Arguments:
- layer_depth: float32 [32, 256, 1024], P(None, 'lat', 'lon'), may hold values from 0.5 to 1.5
- momentum: float32 [2, 32, 256, 1024], P(None, None, 'lat', 'lon'), may hold values from -1 to 1
- gravity: float32 [32], replicated, may hold values from 1 to 4
- absorption: float32 [56, 32], replicated, may hold values from 0.003 to 0.06
- solar_flux: float32 [56], replicated, may hold values from 0.125 to 1.25
- cos_zenith: float32 [256, 1024], P('lat', 'lon'), may hold values from 0.05 to 1
- sunlit: int32 [256, 8], P('lat', 'lon'), may hold values from 0 to 1
- owner_index: int32 [256, 8], P('lat', 'lon'), may hold values from 0 to 7, as said below
- slot_index: int32 [256, 8], P('lat', 'lon'), may hold values from 0 to 7, as said below
- received_counts: int32 [4, 8, 8], P('lat', 'lon'), may hold values from 0 to 8, as said below
Outputs:
- depth_out: float32 [32, 256, 1024], P(None, 'lat', 'lon')
- momentum_out: float32 [2, 32, 256, 1024], P(None, None, 'lat', 'lon')
- heating: float32 [32, 256, 1024], P(None, 'lat', 'lon')
- ledger: float32 [4, 8, 32], P('lat', 'lon')
Inputs may be any that keep to these rules, and one draw needn't show every extreme that they name: For dark blocks owner_index is the block's own lon index and slot_index is 0; sunlit blocks of one device go to distinct (owner, slot) pairs. `slot_index`: the slots of the blocks that one device hands to one owner are 0, 1, ... without gaps. received_counts agrees with sunlit and owner_index; each owner receives at most 32 blocks in all from its lat index.
All inputs are finite; a program needn't handle non-finite values.
Results may differ from a plain program's by a relative error of at most 0.00014.
Values sent between devices are 32-bit elements; how exact they have to be, the bound alone decides.
No kernel may reach another device: no remote copies, remote signals or barrier semaphores. Data moves between devices by JAX's collectives and lax.ppermute only.
A program may use at most 128 MiB of HBM per device.

v0:
```python
import jax
import jax.numpy as jnp
from jax import lax
from jax.sharding import PartitionSpec as P

STEPS = 2


COURANT = 0.06
CORIOLIS = 0.08
LAT_START = 0.35
LAT_SPAN = 0.62
LAYER_GROUP = 8


def padded_2(x, sides, width):
    for axis, dim in sides:
        peers, length = (lax.axis_size(axis), x.shape[dim])
        up = [(i, (i + 1) % peers) for i in range(peers)]
        down = [(j, i) for i, j in up]
        last = lax.slice_in_dim(x, length - width, length, axis=dim)
        initial = lax.slice_in_dim(x, 0, width, axis=dim)
        before = lax.ppermute(last, axis, up)
        after = lax.ppermute(initial, axis, down)
        x = jnp.concatenate([before, x, after], axis=dim)
    return x


def physical_flux(state, velocity, gravity, along_axis):
    column_depth = state[0]
    normal = state[along_axis]
    other_mom = state[3 - along_axis]
    push_flux = normal * velocity + 0.5 * gravity * column_depth * column_depth
    carry_flux = other_mom * velocity
    if along_axis == 1:
        return jnp.stack([normal, push_flux, carry_flux])
    return jnp.stack([normal, carry_flux, push_flux])


def hll_flux(left_state, right_state, gravity, along_axis):
    velocity_left = left_state[along_axis] / left_state[0]
    velocity_right = right_state[along_axis] / right_state[0]
    wave_left = jnp.sqrt(gravity * left_state[0])
    wave_right = jnp.sqrt(gravity * right_state[0])
    lower_wave = jnp.minimum(
        jnp.minimum(velocity_left - wave_left, velocity_right - wave_right), 0.0
    )
    upper_wave = jnp.maximum(
        jnp.maximum(velocity_left + wave_left, velocity_right + wave_right), 0.0
    )
    flux_left = physical_flux(left_state, velocity_left, gravity, along_axis)
    flux_right = physical_flux(right_state, velocity_right, gravity, along_axis)
    return (
        upper_wave * flux_left
        - lower_wave * flux_right
        + lower_wave * upper_wave * (right_state - left_state)
    ) / (upper_wave - lower_wave)


def advance(padded, gravity, latitude):
    centre = padded[:, :, 1:-1, 1:-1]
    east_flux = hll_flux(padded[:, :, 1:-1, :-1], padded[:, :, 1:-1, 1:], gravity, 1)
    north_flux = hll_flux(padded[:, :, :-1, 1:-1], padded[:, :, 1:, 1:-1], gravity, 2)
    cos_centre = jnp.cos(latitude[1:-1])[:, None]
    cos_face = jnp.cos(0.5 * (latitude[:-1] + latitude[1:]))[:, None]
    change = (
        east_flux[..., 1:]
        - east_flux[..., :-1]
        + cos_face[1:] * north_flux[:, :, 1:]
        - cos_face[:-1] * north_flux[:, :, :-1]
    )
    updated = centre - COURANT / cos_centre * change
    turning = CORIOLIS * jnp.sin(latitude[1:-1])[:, None]
    return jnp.stack(
        [updated[0], updated[1] + turning * updated[2], updated[2] - turning * updated[1]]
    )


def shortwave(column_depth, column_sun, absorption, solar_flux):
    layers = column_depth.shape[0]
    sun_cos = column_sun[None]
    top_flux = solar_flux[:, None, None] * sun_cos

    def add_block(block_number, carry):
        path, above, absorbed = carry
        begin = block_number * LAYER_GROUP
        depth_block = lax.dynamic_slice_in_dim(column_depth, begin, LAYER_GROUP, 0)
        absorb_block = lax.dynamic_slice_in_dim(absorption, begin, LAYER_GROUP, 1)
        layer_rows = []
        for inner in range(LAYER_GROUP):
            path = path + absorb_block[:, inner][:, None, None] * depth_block[inner][None]
            down = top_flux * jnp.exp(-path / sun_cos)
            layer_rows.append(jnp.sum(above - down, axis=0))
            above = down
        absorbed = lax.dynamic_update_slice_in_dim(absorbed, jnp.stack(layer_rows), begin, 0)
        return (path, above, absorbed)

    start = (
        jnp.zeros(top_flux.shape, jnp.float32),
        top_flux,
        jnp.zeros(column_depth.shape, jnp.float32),
    )
    absorbed = lax.fori_loop(0, layers // LAYER_GROUP, add_block, start)[2]
    return (absorbed / column_depth, absorbed)


def packed_positions(block_counts, loaded_slot_table, slot_capacity):
    count_ends = jnp.cumsum(block_counts)
    starts = count_ends - block_counts
    slot_order = jnp.arange(loaded_slot_table)
    source_of = jnp.minimum(
        jnp.sum((count_ends[None, :] <= slot_order[:, None]).astype(jnp.int32), axis=1),
        block_counts.shape[0] - 1,
    )
    slot_place = jnp.clip(slot_order - jnp.take(starts, source_of), 0, slot_capacity - 1)
    valid_mask = slot_order < jnp.sum(block_counts)
    target = source_of * slot_capacity + slot_place
    all_slots = block_counts.shape[0] * slot_capacity
    slot_mapping = (
        (jnp.arange(all_slots)[:, None] == target[None, :]) & valid_mask[None, :]
    ).astype(jnp.float32)
    return (slot_mapping, valid_mask)


def clamp_edges(padded, rim_width, at_first, at_final):
    top_edge = padded[:, :, rim_width : rim_width + 1]
    bottom_edge = padded[:, :, -rim_width - 1 : -rim_width]
    head_rows = jnp.where(at_first, top_edge, padded[:, :, :rim_width])
    tail_rows = jnp.where(at_final, bottom_edge, padded[:, :, -rim_width:])
    return jnp.concatenate([head_rows, padded[:, :, rim_width:-rim_width], tail_rows], axis=2)


def latitudes(row_start, band_rows, rim_width, total_rows):
    positions = (row_start + jnp.arange(-rim_width, band_rows + rim_width)).astype(jnp.float32)
    return LAT_START + (positions + 0.5) * (LAT_SPAN / total_rows)


def body(
    layer_depth,
    momentum,
    gravity,
    absorption,
    solar_flux,
    cos_zenith,
    sunlit,
    owner_index,
    slot_index,
    received_counts,
):
    band_rows = layer_depth.shape[1]
    slot_capacity = band_rows // lax.axis_size("lon")
    loaded_slot_table = band_rows // 2
    lit_rows = sunlit[:, 0]
    target_row = owner_index[:, 0] * slot_capacity + slot_index[:, 0]
    placement = (
        (target_row[:, None] == jnp.arange(band_rows)[None, :]) & (lit_rows[:, None] == 1)
    ).astype(jnp.float32)
    slot_mapping, valid_mask = packed_positions(
        received_counts[0, 0], loaded_slot_table, slot_capacity
    )
    highest = lax.Precision.HIGHEST
    heating_part, absorbed = shortwave(layer_depth, cos_zenith, absorption, solar_flux)
    lit_float = lit_rows.astype(jnp.float32)
    heating = heating_part * lit_float[None, :, None]
    row_means = jnp.mean(absorbed, axis=(0, 2)) * lit_float
    outgoing = jnp.dot(row_means, placement, precision=highest)
    arrived = lax.all_to_all(outgoing, "lon", split_axis=0, concat_axis=0, tiled=True)
    ledger = jnp.dot(arrived, slot_mapping, precision=highest)
    state = jnp.stack([layer_depth, momentum[0], momentum[1]])
    weight = gravity.reshape(-1, 1, 1)
    total_rows = band_rows * lax.axis_size("lat")
    row_start = lax.axis_index("lat") * band_rows
    at_first = lax.axis_index("lat") == 0
    at_final = lax.axis_index("lat") == lax.axis_size("lat") - 1
    for step_number in range(STEPS):
        padded = padded_2(state, (("lon", 3), ("lat", 2)), 1)
        state = advance(
            clamp_edges(padded, 1, at_first, at_final),
            weight,
            latitudes(row_start, band_rows, 1, total_rows),
        )
    return (state[0], state[1:], heating, ledger[None, None])


def solution(mesh):
    placed = (
        P(None, "lat", "lon"),
        P(None, None, "lat", "lon"),
        P(),
        P(),
        P(),
        P("lat", "lon"),
        P("lat", "lon"),
        P("lat", "lon"),
        P("lat", "lon"),
        P("lat", "lon", None),
    )
    return jax.shard_map(
        body,
        mesh=mesh,
        in_specs=placed,
        out_specs=(
            P(None, "lat", "lon"),
            P(None, None, "lat", "lon"),
            P(None, "lat", "lon"),
            P("lat", "lon", None),
        ),
        check_vma=False,
    )
```

profile of v0, /device:TPU:1, one launch (start us, length us, event | category | flops | bytes accessed | tf_op | source)
XLA Modules:
  0.0 366.3 jit_solution(12689947796337147681)
XLA Ops:
  17.1 38.2 %while.18 = (s32[]{:T(128)}, f32[56,64,128]{2,1,0:T(8,128)S(1)}, f32[56,64,128]{2,1,0:T(8,128)}, f32[32,64,128]{2,1,0:T(8,128)}, f32[56,32]{0,1:T(8,128)}, /*ind...) while((s32[]{:T(128)}, f32[56,64,128]{2,1,0:T(8,128)S(1)}, ...), condition=%wide.region_9.10_spmd.clone, body=%wide.region_0.9_spmd.clone.sunk | while | flops 30670860 | bytes 29829132 | solution.py:103
  59.1 5.7 %all-to-all-start = ((f32[8,8,1]{1,2,0:T(1,128)}), f32[8,8,1]{1,2,0:T(1,128)S(1)}, u32[]{:S(2)}, u32[]{:S(2)}) async-start(f32[8,8,1]{1,2,0:T(1,128)} %convolution_bitcast_fusion), calls=%async_computation | async-start | bytes 8192 | tf_op jit(solution)/shard_map/all_to_all | solution.py:167
  75.9 11.1 %fusion.50 = (f32[3,32,1,130]{2,1,3,0:T(8,128)}, f32[3,32,1,130]{2,1,3,0:T(8,128)}) fusion(f32[3,32,64,130]{2,1,3,0:T(8,128)} %pad_maximum_fusion.1), kind=kLoop, calls=%fused_computation.213 | loop fusion | bytes 199680 | tf_op jit(solution)/shard_map/slice | solution.py:126
  87.0 6.5 %copy.31 = f32[3,32,1,130]{3,1,2,0:T(8,128)S(1)} copy(f32[3,32,1,130]{2,1,3,0:T(8,128)} %get-tuple-element.281) | data formatting | bytes 99840 | tf_op jit(solution)/shard_map/slice | solution.py:126
  96.2 6.5 %copy.29 = f32[3,32,1,130]{3,1,2,0:T(8,128)S(1)} copy(f32[3,32,1,130]{2,1,3,0:T(8,128)} %get-tuple-element.282) | data formatting | bytes 99840 | tf_op jit(solution)/shard_map/slice | solution.py:21
  117.5 7.2 %fusion.24 = (f32[1,32,64,129]{2,1,3,0:T(8,128)}, f32[1,32,64,129]{2,1,3,0:T(8,128)}, f32[1,32,64,129]{2,1,3,0:T(8,128)}, f32[1,32,64,129]{2,1,3,0:T(8,128)}, f3...) fusion(f32[1,32,64,129]{2,1,3,0:T(8,128)} %get-tuple-element.229, f32[3,32,64,129]{2,1,3,0:T(8,128)S(1)} %get-tuple-element.297, ...), kind=kLoop, calls=%fused_computation.119 | loop fusion | flops 2641920 | bytes 14794880 | tf_op jit(solution)/shard_map/add | solution.py:33
  124.7 10.3 %fusion.4 = f32[3,32,64,129]{2,1,3,0:T(8,128)} fusion(f32[1,32,64,129]{2,1,3,0:T(8,128)} %get-tuple-element.266, f32[1,32,64,129]{2,1,3,0:T(8,128)} %get-tuple-element.265, f32[1,32,64,129]{2,1,3,0:T(8,128)} %get-tuple-element.286, f32[1,32,64,129]{2,1,3,0:T(8,128)} %get-tuple-element.304, f32[1,32,64,129]{2,1,3,0:T(8,128)} %get-tuple-element.305, ...), kind=kLoop, calls=%fused_computation.68 | loop fusion | flops 11888640 | bytes 16932864 | tf_op jit(solution)/shard_map/div | solution.py:53
  135.0 8.1 %copy.32 = f32[3,32,1,130]{2,1,3,0:T(8,128)} copy(f32[3,32,1,130]{3,1,2,0:T(8,128)S(1)} %collective-permute-done.3) | data formatting | bytes 99840 | tf_op jit(solution)/shard_map/ppermute | solution.py:24
  143.1 8.1 %copy.30 = f32[3,32,1,130]{2,1,3,0:T(8,128)} copy(f32[3,32,1,130]{3,1,2,0:T(8,128)S(1)} %collective-permute-done.2) | data formatting | bytes 99840 | tf_op jit(solution)/shard_map/ppermute | solution.py:23
  151.2 15.1 %broadcast_select_fusion.1 = (f32[3,32,1,130]{2,1,3,0:T(8,128)}, f32[3,32,1,130]{2,1,3,0:T(8,128)}) fusion(f32[3,32,1,130]{2,1,3,0:T(8,128)} %copy.32, pred[]{:T(512)S(6)} %eq.57, f32[3,32,64,130]{2,1,3,0:T(8,128)} %pad_maximum_fusion.1, f32[3,32,1,130]{2,1,3,0:T(8,128)} %copy.30, pred[]{:T(512)S(6)} %eq.56), kind=kLoop, calls=%fused_computation.108 | loop fusion | flops 24960 | bytes 299522 | tf_op jit(solution)/shard_map/jit(_where)/select_n | solution.py:129
  166.3 9.2 %pad_maximum_fusion.2 = (f32[3,32,65,130]{2,1,3,0:T(8,128)S(1)}, f32[3,32,65,130]{2,1,3,0:T(8,128)}) fusion(f32[3,32,1,130]{2,1,3,0:T(8,128)} %get-tuple-element.279, f32[3,32,64,1]{2,1,3,0:T(8,128)S(1)} %collective-permute-done.1, f32[2,32,64,128]{2,1,3,0:T(8,128)S(1)} %copy-done.1, f32[1,32,64,128]{2,1,3,0:T(8,128)S(1)} %bitcast.140, ...), kind=kLoop, calls=%fused_computation.59 | loop fusion | flops 6489600 | bytes 9784320 | tf_op jit(solution)/shard_map/concatenate | solution.py:130
  187.3 10.6 %fusion.21 = f32[3,32,65,128]{2,1,3,0:T(8,128)} fusion(f32[3,32,65,130]{2,1,3,0:T(8,128)S(1)} %bitcast.143, f32[3,32,65,130]{2,1,3,0:T(8,128)S(1)} %get-tuple-element.277, f32[1,32,65,128]{2,1,3,0:T(8,128)} %get-tuple-element.313, f32[1,32,65,128]{2,1,3,0:T(8,128)} %get-tuple-element.314, f32[1,32,65,128]{2,1,3,0:T(8,128)} %get-tuple-element.276, ...), kind=kLoop, calls=%fused_computation.97 | loop fusion | flops 8785920 | bytes 20234240 | tf_op jit(solution)/shard_map/div | solution.py:53
  197.9 10.3 %fusion.8 = f32[3,32,64,128]{2,1,3,0:T(8,128)S(1)} fusion(f32[2,32,64,128]{2,1,3,0:T(8,128)S(1)} %copy-done.1, f32[1,32,64,128]{2,1,3,0:T(8,128)S(1)} %bitcast.141, f32[3,32,65,128]{2,1,3,0:T(8,128)} %fusion.21, f32[3,32,64,129]{2,1,3,0:T(8,128)} %fusion.4, f32[64]{0:T(128)S(1)} %get-tuple-element.315, f32[64]{0:T(128)S(1)} %get-tuple-element.316, ...), kind=kLoop, calls=%fused_computation.77 | loop fusion | flops 6291456 | bytes 18875136 | tf_op jit(solution)/shard_map/sub | solution.py:72
  219.4 11.1 %fusion.49 = (f32[3,32,1,130]{2,1,3,0:T(8,128)}, f32[3,32,1,130]{2,1,3,0:T(8,128)}) fusion(f32[3,32,64,130]{2,1,3,0:T(8,128)} %pad_maximum_fusion.3), kind=kLoop, calls=%fused_computation.212 | loop fusion | bytes 199680 | tf_op jit(solution)/shard_map/slice | solution.py:126
  230.5 6.5 %copy.35 = f32[3,32,1,130]{3,1,2,0:T(8,128)S(1)} copy(f32[3,32,1,130]{2,1,3,0:T(8,128)} %get-tuple-element.273) | data formatting | bytes 99840 | tf_op jit(solution)/shard_map/slice | solution.py:126
  237.0 6.5 %copy.33 = f32[3,32,1,130]{3,1,2,0:T(8,128)S(1)} copy(f32[3,32,1,130]{2,1,3,0:T(8,128)} %get-tuple-element.274) | data formatting | bytes 99840 | tf_op jit(solution)/shard_map/slice | solution.py:21
  255.6 7.5 %fusion.26 = (f32[1,32,64,129]{2,1,3,0:T(8,128)}, f32[1,32,64,129]{2,1,3,0:T(8,128)}, f32[1,32,64,129]{2,1,3,0:T(8,128)}, f32[1,32,64,129]{2,1,3,0:T(8,128)}, f3...) fusion(f32[1,32,64,129]{2,1,3,0:T(8,128)} %get-tuple-element.219, f32[3,32,64,129]{2,1,3,0:T(8,128)S(1)} %get-tuple-element.292, ...), kind=kLoop, calls=%fused_computation.121 | loop fusion | flops 2641920 | bytes 14794880 | tf_op jit(solution)/shard_map/add | solution.py:33
  266.0 8.9 %fusion.7 = f32[3,32,64,129]{2,1,3,0:T(8,128)} fusion(f32[1,32,64,129]{2,1,3,0:T(8,128)} %get-tuple-element.262, f32[1,32,64,129]{2,1,3,0:T(8,128)} %get-tuple-element.261, f32[1,32,64,129]{2,1,3,0:T(8,128)} %get-tuple-element.284, f32[1,32,64,129]{2,1,3,0:T(8,128)} %get-tuple-element.307, f32[1,32,64,129]{2,1,3,0:T(8,128)} %get-tuple-element.308, ...), kind=kLoop, calls=%fused_computation.75 | loop fusion | flops 13473792 | bytes 16932864 | tf_op jit(solution)/shard_map/div | solution.py:53
  274.9 8.0 %copy.36 = f32[3,32,1,130]{2,1,3,0:T(8,128)} copy(f32[3,32,1,130]{3,1,2,0:T(8,128)S(1)} %collective-permute-done.7) | data formatting | bytes 99840 | tf_op jit(solution)/shard_map/ppermute | solution.py:24
  282.9 8.0 %copy.34 = f32[3,32,1,130]{2,1,3,0:T(8,128)} copy(f32[3,32,1,130]{3,1,2,0:T(8,128)S(1)} %collective-permute-done.6) | data formatting | bytes 99840 | tf_op jit(solution)/shard_map/ppermute | solution.py:23
  290.9 15.2 %broadcast_select_fusion = (f32[3,32,1,130]{2,1,3,0:T(8,128)}, f32[3,32,1,130]{2,1,3,0:T(8,128)}) fusion(f32[3,32,1,130]{2,1,3,0:T(8,128)} %copy.36, pred[]{:T(512)S(6)} %eq.57, f32[3,32,64,130]{2,1,3,0:T(8,128)} %pad_maximum_fusion.3, f32[3,32,1,130]{2,1,3,0:T(8,128)} %copy.34, pred[]{:T(512)S(6)} %eq.56), kind=kLoop, calls=%fused_computation.107 | loop fusion | flops 24960 | bytes 299522 | tf_op jit(solution)/shard_map/jit(_where)/select_n | solution.py:129
  306.1 10.6 %pad_maximum_fusion.4 = (f32[3,32,65,130]{2,1,3,0:T(8,128)S(1)}, f32[3,32,65,130]{2,1,3,0:T(8,128)}) fusion(f32[3,32,1,130]{2,1,3,0:T(8,128)} %get-tuple-element.271, f32[3,32,64,1]{2,1,3,0:T(8,128)S(1)} %collective-permute-done.5, f32[1,32,64,128]{2,1,3,0:T(8,128)S(1)} %copy-done.6, f32[1,32,64,128]{2,1,3,0:T(8,128)S(1)} %get-tuple-element.289, ...), kind=kLoop, calls=%fused_computation.62 | loop fusion | flops 8112000 | bytes 9784320 | tf_op jit(solution)/shard_map/concatenate | solution.py:130
  330.1 10.9 %fusion.15 = f32[3,32,65,128]{2,1,3,0:T(8,128)} fusion(f32[3,32,65,130]{2,1,3,0:T(8,128)S(1)} %copy-done.10, f32[3,32,65,130]{2,1,3,0:T(8,128)S(1)} %get-tuple-element.269, f32[1,32,65,128]{2,1,3,0:T(8,128)} %get-tuple-element.254, f32[1,32,65,128]{2,1,3,0:T(8,128)} %get-tuple-element.253, f32[1,32,65,128]{2,1,3,0:T(8,128)} %get-tuple-element.268, ...), kind=kLoop, calls=%fused_computation.87 | loop fusion | flops 8785920 | bytes 20234240 | tf_op jit(solution)/shard_map/div | solution.py:53
  341.0 10.5 %fusion.11 = f32[3,32,64,128]{2,1,3,0:T(8,128)S(1)} fusion(f32[3,32,65,128]{2,1,3,0:T(8,128)} %fusion.15, f32[3,32,64,129]{2,1,3,0:T(8,128)} %fusion.7, f32[64]{0:T(128)S(1)} %get-tuple-element.315, f32[64]{0:T(128)S(1)} %get-tuple-element.316, f32[64]{0:T(128)S(1)} %get-tuple-element.310, f32[1,32,64,128]{2,1,3,0:T(8,128)S(1)} %copy-done.6, ...), kind=kLoop, calls=%fused_computation.81 | loop fusion | flops 7077888 | bytes 18875136 | tf_op jit(solution)/shard_map/sub | solution.py:72
  (189 shorter events, 152.4 us)
Async XLA Ops:
  0.6 5.6 %copy-start.14 = (f32[32,64,128]{2,1,0:T(8,128)S(1)}, f32[32,64,128]{2,1,0:T(8,128)}, u32[]{:S(2)}) copy-start(f32[32,64,128]{2,1,0:T(8,128)} %param.12) | copy-start | bytes 3145732
  8.1 6.4 %copy-start.21 = (s32[64,1]{0,1:T(1,128)S(1)}, s32[64,1]{0,1:T(1,128)}, u32[]{:S(2)}) copy-start(s32[64,1]{0,1:T(1,128)} %param.18) | copy-start | bytes 772
  8.1 6.4 %copy-start.13 = (f32[64,128]{1,0:T(8,128)S(1)}, f32[64,128]{1,0:T(8,128)}, u32[]{:S(2)}) copy-start(f32[64,128]{1,0:T(8,128)} %param.17) | copy-start | bytes 98308
  8.1 6.4 %copy-start.17 = (f32[56]{0:T(128)S(1)}, f32[56]{0:T(128)}, u32[]{:S(2)}) copy-start(f32[56]{0:T(128)} %param.16) | copy-start | bytes 676
  9.4 61.9 %collective-permute-start.1 = (f32[3,32,64,1]{2,1,3,0:T(8,128)S(1)}, f32[3,32,64,1]{2,1,3,0:T(8,128)S(1)}, u32[]{:S(2)}, u32[]{:S(2)}) collective-permute-start(f32[3,32,64,1]{2,1,3,0:T(8,128)S(1)} %get-tuple-element.300), channel_id=1, source_target_pairs={{4,0},{8,4},{12,8},{16,12},{20,16},{24,20},{28,24},{0,28},{5,1},{9... | collective-permute-start | bytes 73736 | tf_op jit(solution)/shard_map/ppermute | solution.py:24
  14.5 56.7 %collective-permute-start = (f32[3,32,64,1]{2,1,3,0:T(8,128)S(1)}, f32[3,32,64,1]{2,1,3,0:T(8,128)S(1)}, u32[]{:S(2)}, u32[]{:S(2)}) collective-permute-start(f32[3,32,64,1]{2,1,3,0:T(8,128)S(1)} %get-tuple-element.299), channel_id=1, source_target_pairs={{0,4},{4,8},{8,12},{12,16},{16,20},{20,24},{24,28},{28,0},{1,5},{5... | collective-permute-start | bytes 73736 | tf_op jit(solution)/shard_map/ppermute | solution.py:23
  55.3 9.5 %copy-start.18 = (f32[32]{0:T(128)S(1)}, f32[32]{0:T(128)}, u32[]{:S(2)}) copy-start(f32[32]{0:T(128)} %param.14) | copy-start | bytes 388
  55.3 9.8 %copy-start.22 = (s32[1,1,8]{2,1,0:T(1,128)S(1)}, s32[1,1,8]{2,1,0:T(1,128)}, u32[]{:S(2)}) copy-start(s32[1,1,8]{2,1,0:T(1,128)} %param.21) | copy-start | bytes 100
  55.3 16.0 %copy-start.3 = (f32[32,64,128]{1,0,2:T(8,128)S(1)}, f32[32,64,128]{1,0,2:T(8,128)}, u32[]{:S(2)}) copy-start(f32[32,64,128]{1,0,2:T(8,128)} %copy-done.2) | copy-start | bytes 3145732
  59.1 11.0 %all-to-all-start = ((f32[8,8,1]{1,2,0:T(1,128)}), f32[8,8,1]{1,2,0:T(1,128)S(1)}, u32[]{:S(2)}, u32[]{:S(2)}) async-start(f32[8,8,1]{1,2,0:T(1,128)} %convolution_bitcast_fusion), calls=%async_computation | async-start | bytes 8192 | tf_op jit(solution)/shard_map/all_to_all | solution.py:167
  93.5 41.5 %collective-permute-start.3 = (f32[3,32,1,130]{3,1,2,0:T(8,128)S(1)}, f32[3,32,1,130]{3,1,2,0:T(8,128)S(1)}, u32[]{:S(2)}, u32[]{:S(2)}) collective-permute-start(f32[3,32,1,130]{3,1,2,0:T(8,128)S(1)} %copy.31), channel_id=1, source_target_pairs={{1,0},{2,1},{3,2},{0,3},{5,4},{6,5},{7,6},{4,7},{9,8},{10,9},{11,1... | collective-permute-start | bytes 149768 | tf_op jit(solution)/shard_map/ppermute | solution.py:24
  102.7 40.4 %collective-permute-start.2 = (f32[3,32,1,130]{3,1,2,0:T(8,128)S(1)}, f32[3,32,1,130]{3,1,2,0:T(8,128)S(1)}, u32[]{:S(2)}, u32[]{:S(2)}) collective-permute-start(f32[3,32,1,130]{3,1,2,0:T(8,128)S(1)} %copy.29), channel_id=1, source_target_pairs={{0,1},{1,2},{2,3},{3,0},{4,5},{5,6},{6,7},{7,4},{8,9},{9,10},{10,1... | collective-permute-start | bytes 149768 | tf_op jit(solution)/shard_map/ppermute | solution.py:23
  117.5 7.2 %copy-start = (f32[2,32,64,128]{2,1,3,0:T(8,128)S(1)}, f32[2,32,64,128]{2,1,3,0:T(8,128)}, u32[]{:S(2)}) copy-start(f32[2,32,64,128]{2,1,3,0:T(8,128)} %copy.28) | copy-start | bytes 6291460
  151.2 15.1 %copy-start.1 = (f32[2,32,64,128]{2,1,3,0:T(8,128)S(1)}, f32[2,32,64,128]{2,1,3,0:T(8,128)}, u32[]{:S(2)}) copy-start(f32[2,32,64,128]{2,1,3,0:T(8,128)} %copy.28) | copy-start | bytes 6291460
  209.0 7.3 %copy-start.4 = (f32[1,32,64,128]{2,1,3,0:T(8,128)}, f32[1,32,64,128]{2,1,3,0:T(8,128)S(1)}, u32[]{:S(2)}) copy-start(f32[1,32,64,128]{2,1,3,0:T(8,128)S(1)} %get-tuple-element.290) | copy-start | bytes 3145732
  209.0 7.3 %copy-start.7 = (f32[1,32,64,128]{2,1,3,0:T(8,128)}, f32[1,32,64,128]{2,1,3,0:T(8,128)S(1)}, u32[]{:S(2)}) copy-start(f32[1,32,64,128]{2,1,3,0:T(8,128)S(1)} %get-tuple-element.296) | copy-start | bytes 3145732
  209.9 3.2 collective-permute-start.5
  210.7 5.6 %collective-permute-start.4 = (f32[3,32,64,1]{2,1,3,0:T(8,128)S(1)}, f32[3,32,64,1]{2,1,3,0:T(8,128)S(1)}, u32[]{:S(2)}, u32[]{:S(2)}) collective-permute-start(f32[3,32,64,1]{2,1,3,0:T(8,128)S(1)} %get-tuple-element.294), channel_id=1, source_target_pairs={{0,4},{4,8},{8,12},{12,16},{16,20},{20,24},{24,28},{28,0},{1,5},{5... | collective-permute-start | bytes 73736 | tf_op jit(solution)/shard_map/ppermute | solution.py:23
  237.0 37.9 %collective-permute-start.7 = (f32[3,32,1,130]{3,1,2,0:T(8,128)S(1)}, f32[3,32,1,130]{3,1,2,0:T(8,128)S(1)}, u32[]{:S(2)}, u32[]{:S(2)}) collective-permute-start(f32[3,32,1,130]{3,1,2,0:T(8,128)S(1)} %copy.35), channel_id=1, source_target_pairs={{1,0},{2,1},{3,2},{0,3},{5,4},{6,5},{7,6},{4,7},{9,8},{10,9},{11,1... | collective-permute-start | bytes 149768 | tf_op jit(solution)/shard_map/ppermute | solution.py:24
  243.5 39.4 %collective-permute-start.6 = (f32[3,32,1,130]{3,1,2,0:T(8,128)S(1)}, f32[3,32,1,130]{3,1,2,0:T(8,128)S(1)}, u32[]{:S(2)}, u32[]{:S(2)}) collective-permute-start(f32[3,32,1,130]{3,1,2,0:T(8,128)S(1)} %copy.33), channel_id=1, source_target_pairs={{0,1},{1,2},{2,3},{3,0},{4,5},{5,6},{6,7},{7,4},{8,9},{9,10},{10,1... | collective-permute-start | bytes 149768 | tf_op jit(solution)/shard_map/ppermute | solution.py:23
  255.6 7.5 %copy-start.12 = (f32[1,32,64,129]{2,1,3,0:T(8,128)S(1)}, f32[1,32,64,129]{2,1,3,0:T(8,128)}, u32[]{:S(2)}) copy-start(f32[1,32,64,129]{2,1,3,0:T(8,128)} %get-tuple-element.217) | copy-start | bytes 3170308
  290.9 15.2 %copy-start.6 = (f32[1,32,64,128]{2,1,3,0:T(8,128)S(1)}, f32[1,32,64,128]{2,1,3,0:T(8,128)}, u32[]{:S(2)}) copy-start(f32[1,32,64,128]{2,1,3,0:T(8,128)} %copy-done.4) | copy-start | bytes 3145732
  290.9 15.2 %copy-start.9 = (f32[1,32,64,128]{2,1,3,0:T(8,128)S(1)}, f32[1,32,64,128]{2,1,3,0:T(8,128)}, u32[]{:S(2)}) copy-start(f32[1,32,64,128]{2,1,3,0:T(8,128)} %copy-done.7) | copy-start | bytes 3145732
  316.7 5.5 %copy-start.10 = (f32[3,32,65,130]{2,1,3,0:T(8,128)S(1)}, f32[3,32,65,130]{2,1,3,0:T(8,128)}, u32[]{:S(2)}) copy-start(f32[3,32,65,130]{2,1,3,0:T(8,128)} %get-tuple-element.270) | copy-start | bytes 9734404
  (13 other events, 46.2 us)
where the time goes:
time: 372 us; the launch traced here: 366 us
  other arithmetic  227 us (61%)
  local copies, waits for them, and re-layouts  111 us (30%)
  starting transfers between devices  18.2 us (5%)
  waiting for transfers between devices  6.84 us (2%)
    div x8, other arithmetic, hll_flux(): (upper_wave * flux_left - lower_wave * flux_right + lower_wave * upper_wa...  48.5 us
    slice x4, local copies, waits for them, and re-layouts, clamp_edges(): top_edge = padded[:, :, rim_width:rim_width + 1]  35.2 us
    select_n x2, other arithmetic, clamp_edges(): tail_rows = jnp.where(at_final, bottom_edge, padded[:, :, -rim_width:])  30.3 us
    reduce_sum x8, other arithmetic, add_block(): layer_rows.append(jnp.sum(above - down, axis=0))  26.4 us
    mul x4, other arithmetic, hll_flux(): lower_wave * upper_wave * (right_state - left_state)  21 us
    sub x2, other arithmetic, advance(): updated = centre - COURANT / cos_centre * change  20.8 us
    concatenate x2, other arithmetic, clamp_edges(): jnp.concatenate([head_rows, padded[:, :, rim_width:-rim_width], tail_rows...  19.8 us
    concatenate x4, other arithmetic, padded_2(): x = jnp.concatenate([before, x, after], axis=dim)  17.8 us
  transfers between devices with their start and end apart: 9, of which 3 were waited for; matrix products, arithmetic and copies ran while one was open for 37% of the time, Pallas kernels for 0%

commit v1 on v0

v1 whole, which is shorter than its diff:
```python
import functools
import math

import jax
import jax.numpy as jnp
import numpy as np
from jax import lax
from jax.experimental import pallas as pl
from jax.experimental.pallas import tpu as pltpu
from jax.sharding import PartitionSpec as P

COURANT = 0.06
CORIOLIS = 0.08
LAT_START = 0.35
LAT_SPAN = 0.62
LANES = 128
SUB = 8
SUN_ROWS = 16
SUN_BANDS = 14
VMEM_LIMIT = 48 * 1024 * 1024


def params(**more):
    return pltpu.CompilerParams(vmem_limit_bytes=VMEM_LIMIT, **more)


def lane_index(rows=SUB):
    return lax.broadcasted_iota(jnp.int32, (rows, LANES), 1)


def latitude_table(lat_parts, band_rows):
    total = lat_parts * band_rows
    rows = np.arange(lat_parts)[:, None] * band_rows + np.arange(-2, LANES)[None, :]
    latitude = np.float32(LAT_START) + (rows.astype(np.float32) + np.float32(0.5)) * np.float32(LAT_SPAN / total)
    face = (np.float32(0.5) * (latitude[:, :-1] + latitude[:, 1:])).astype(np.float64)
    latitude = latitude.astype(np.float64)
    table = np.zeros((lat_parts, 8, LANES), np.float32)
    table[:, 0] = COURANT / np.cos(latitude[:, 1 : LANES + 1])
    table[:, 1] = np.cos(face[:, 1 : LANES + 1])
    table[:, 2] = np.cos(face[:, :LANES])
    table[:, 3] = CORIOLIS * np.sin(latitude[:, 1 : LANES + 1])
    return table.reshape(lat_parts * 8, LANES)


def cell(depth, east_mom, north_mom, gravity):
    inverse = 1.0 / depth
    east_vel = east_mom * inverse
    north_vel = north_mom * inverse
    weight = gravity * depth
    wave = weight * lax.rsqrt(weight)
    push = 0.5 * weight * depth
    cross = north_mom * east_vel
    return (
        depth,
        east_mom,
        north_mom,
        east_vel - wave,
        east_vel + wave,
        east_mom * east_vel + push,
        cross,
        north_vel - wave,
        north_vel + wave,
        north_mom * north_vel + push,
    )


def east_side(c):
    return (c[0], c[1], c[2], c[3], c[4], c[5], c[6])


def north_side(c):
    return (c[0], c[2], c[1], c[7], c[8], c[9], c[6])


def face(left, right):
    lower = jnp.minimum(jnp.minimum(left[3], right[3]), 0.0)
    upper = jnp.maximum(jnp.maximum(left[4], right[4]), 0.0)
    share = upper / (upper - lower)
    rise = right[1] - left[1]
    depth_flux = right[1] + share * (lower * (right[0] - left[0]) - rise)
    normal_flux = right[5] + share * (lower * rise - (right[5] - left[5]))
    other_flux = right[6] + share * (lower * (right[2] - left[2]) - (right[6] - left[6]))
    return depth_flux, normal_flux, other_flux


def turned(state, change, rate, turning):
    depth, east_mom, north_mom = (s - rate * c for s, c in zip(state, change))
    return depth, east_mom + turning * north_mom, north_mom - turning * east_mom


def roll(x, shift):
    return pltpu.roll(x, shift, 1)


def dynamics_kernel(
    band_rows,
    gravity_ref,
    table_ref,
    lanes_ref,
    depth_ref,
    mom_ref,
    north_ref,
    south_ref,
    west_ref,
    east_ref,
    own_west_ref,
    own_east_ref,
    depth_out,
    mom_out,
    middle,
):
    group = pl.program_id(0)
    lat = lax.axis_index("lat")
    at_first = lat == 0
    at_final = lat == lax.axis_size("lat") - 1
    lane = lane_index()
    sublane = lax.broadcasted_iota(jnp.int32, (SUB, LANES), 0)
    gravity = jnp.zeros((SUB, LANES), jnp.float32)
    for i in range(SUB):
        gravity = jnp.where(sublane == i, gravity_ref[group * SUB + i], gravity)

    both = jnp.concatenate([gravity, gravity], axis=0)
    lane2 = lane_index(2 * SUB)
    low_edge = (lane2 == 0) & at_first
    high_edge = (lane2 == band_rows + 1) & at_final

    def column(west, east):
        fields = []
        for f in range(3):
            x = jnp.concatenate([west(f), east(f)], axis=0)
            x = jnp.where(low_edge, roll(x, LANES - 1), x)
            fields.append(jnp.where(high_edge, roll(x, 1), x))
        return cell(*fields, both)

    columns = [
        column(lambda f: west_ref[f, 1], lambda f: own_east_ref[f, 1]),
        column(lambda f: west_ref[f, 0], lambda f: own_east_ref[f, 0]),
        column(lambda f: own_west_ref[f, 0], lambda f: east_ref[f, 0]),
        column(lambda f: own_west_ref[f, 1], lambda f: east_ref[f, 1]),
    ]
    rate_of, upper_cos, lower_cos, turn_of = (
        jnp.broadcast_to(lanes_ref[pl.ds(lat * 8 + q, 1), :], (2 * SUB, LANES)) for q in range(4)
    )
    fluxes = [face(east_side(a), east_side(b)) for a, b in zip(columns[:-1], columns[1:])]
    moved = []
    for k in (1, 2):
        c = columns[k]
        side = north_side(c)
        upper = face(side, tuple(roll(x, LANES - 1) for x in side))
        upper = (upper[0], upper[2], upper[1])
        change = tuple(
            fluxes[k][i] - fluxes[k - 1][i] + upper_cos * upper[i] - lower_cos * roll(upper[i], 1)
            for i in range(3)
        )
        moved.append(cell(*turned(c[:3], change, rate_of, turn_of), both))
    edge_fluxes = (fluxes[1], face(east_side(moved[0]), east_side(moved[1])))

    is_first_lane = lane == 0
    is_last_lane = lane == LANES - 1

    def advance_row(row, here, above, below_flux, edges):
        j = row + 1
        rate = table_ref[lat * 8, j]
        cos_upper = table_ref[lat * 8 + 1, j]
        turning = table_ref[lat * 8 + 3, j]
        upper = face(north_side(here), north_side(above))
        upper = (cos_upper * upper[0], cos_upper * upper[2], cos_upper * upper[1])
        side = east_side(here)
        flux = face(tuple(roll(x, 1) for x in side), side)
        change = []
        for i in range(3):
            west_edge = roll(edges[i][:SUB], lax.rem(2 * LANES - j, LANES))
            east_edge = roll(edges[i][SUB:], lax.rem(2 * LANES - 1 - j, LANES))
            west_flux = jnp.where(is_first_lane, west_edge, flux[i])
            east_flux = jnp.where(is_last_lane, east_edge, roll(flux[i], LANES - 1))
            change.append((east_flux - west_flux) + (upper[i] - below_flux[i]))
        return turned(here[:3], change, rate, turning), upper

    def weighted(row, below, here):
        cos_lower = table_ref[lat * 8 + 2, row + 1]
        flux = face(north_side(below), north_side(here))
        return cos_lower * flux[0], cos_lower * flux[2], cos_lower * flux[1]

    def block_row(row):
        window = pl.ds(row, SUB, stride=band_rows)
        return cell(depth_ref[window, :], mom_ref.at[0][window, :], mom_ref.at[1][window, :], gravity)

    def halo_row(ref, which, clamped, edge_row):
        window = pl.ds(edge_row, SUB, stride=band_rows)
        inside = (depth_ref[window, :], mom_ref.at[0][window, :], mom_ref.at[1][window, :])
        return cell(*(jnp.where(clamped, inside[f], ref[f, which]) for f in range(3)), gravity)

    def store_middle(row, state):
        for f in range(3):
            middle[f, pl.ds(pl.multiple_of((row + 1) * SUB, SUB), SUB), :] = state[f]

    def middle_row(row):
        window = pl.ds(pl.multiple_of((row + 1) * SUB, SUB), SUB)
        return cell(*(middle[f, window, :] for f in range(3)), gravity)

    edges = edge_fluxes[0]
    below, here = (halo_row(north_ref, which, at_first, 0) for which in (1, 0))
    flux = weighted(-1, below, here)
    above = block_row(0)
    state, flux = advance_row(-1, here, above, flux, edges)
    store_middle(-1, state)

    def first_step(unroll):
        def rows(n, carry):
            here, flux = carry
            for i in range(unroll):
                row = n * unroll + i
                above = block_row(row + 1)
                state, flux = advance_row(row, here, above, flux, edges)
                store_middle(row, state)
                here = above
            return here, flux

        return rows

    unroll = 7 if (band_rows - 1) % 7 == 0 else 1
    here, flux = lax.fori_loop(0, (band_rows - 1) // unroll, first_step(unroll), (above, flux))
    for row, above in (
        (band_rows - 1, halo_row(south_ref, 0, at_final, band_rows - 1)),
        (band_rows, halo_row(south_ref, 1, at_final, band_rows - 1)),
    ):
        state, flux = advance_row(row, here, above, flux, edges)
        store_middle(row, state)
        here = above

    @pl.when(at_first)
    def _():
        for f in range(3):
            middle[f, pl.ds(0, SUB), :] = middle[f, pl.ds(SUB, SUB), :]

    @pl.when(at_final)
    def _():
        for f in range(3):
            middle[f, pl.ds((band_rows + 1) * SUB, SUB), :] = middle[f, pl.ds(band_rows * SUB, SUB), :]

    edges2 = edge_fluxes[1]
    here = middle_row(0)
    flux = weighted(0, middle_row(-1), here)
    unroll2 = 8 if band_rows % 8 == 0 else 1

    def second_step(n, carry):
        here, flux = carry
        for i in range(unroll2):
            row = n * unroll2 + i
            above = middle_row(row + 1)
            state, flux = advance_row(row, here, above, flux, edges2)
            window = pl.ds(row, SUB, stride=band_rows)
            depth_out[window, :] = state[0]
            mom_out.at[0][window, :] = state[1]
            mom_out.at[1][window, :] = state[2]
            here = above
        return here, flux

    lax.fori_loop(0, band_rows // unroll2, second_step, (here, flux))


def dynamics(gravity, table, depth, mom, north, south, west, east, own_west, own_east):
    layers, band_rows = gravity.shape[0], depth.shape[0] // gravity.shape[0]
    block = SUB * band_rows
    smem = pl.BlockSpec(memory_space=pltpu.SMEM)
    whole = pl.BlockSpec(table.shape, lambda g: (0, 0))
    depth_spec = pl.BlockSpec((block, LANES), lambda g: (g, 0))
    mom_spec = pl.BlockSpec((2, block, LANES), lambda g: (0, g, 0))
    halo_spec = pl.BlockSpec((3, 2, SUB, LANES), lambda g: (0, 0, g, 0))
    return pl.pallas_call(
        functools.partial(dynamics_kernel, band_rows),
        grid=(layers // SUB,),
        out_shape=(
            jax.ShapeDtypeStruct(depth.shape, jnp.float32),
            jax.ShapeDtypeStruct(mom.shape, jnp.float32),
        ),
        in_specs=[smem, smem, whole, depth_spec, mom_spec] + [halo_spec] * 6,
        out_specs=(depth_spec, mom_spec),
        scratch_shapes=[pltpu.VMEM((3, (band_rows + 2) * SUB, LANES), jnp.float32)],
        compiler_params=params(),
        cost_estimate=pl.CostEstimate(
            flops=220 * depth.size, bytes_accessed=24 * depth.size, transcendentals=8 * depth.size
        ),
        name="dynamics",
    )(gravity, table, table, depth, mom, north, south, west, east, own_west, own_east)


def rows_kernel(depth_head, depth_tail, mom_head, mom_tail, head_out, tail_out):
    layers = depth_head.shape[0] // SUB
    fields = (
        (depth_head, depth_tail),
        (mom_head.at[0], mom_tail.at[0]),
        (mom_head.at[1], mom_tail.at[1]),
    )
    for f, (head, tail) in enumerate(fields):
        for which in range(2):
            head_out[f, which] = head[pl.ds(which, layers, stride=SUB), :]
            tail_out[f, which] = tail[pl.ds(SUB - 1 - which, layers, stride=SUB), :]


def edge_rows(layer_depth, momentum):
    layers, band_rows, _ = layer_depth.shape

    def kernel(depth_head, depth_tail, mom_head, mom_tail, head_out, tail_out):
        rows_kernel(
            depth_head.reshape(layers * SUB, LANES),
            depth_tail.reshape(layers * SUB, LANES),
            mom_head.reshape(2, layers * SUB, LANES),
            mom_tail.reshape(2, layers * SUB, LANES),
            head_out,
            tail_out,
        )

    final = band_rows // SUB - 1
    out = jax.ShapeDtypeStruct((3, 2, layers, LANES), jnp.float32)
    out_spec = pl.BlockSpec(out.shape, lambda i: (0, 0, 0, 0))
    return pl.pallas_call(
        kernel,
        grid=(1,),
        out_shape=(out, out),
        in_specs=[
            pl.BlockSpec((layers, SUB, LANES), lambda i: (0, 0, 0)),
            pl.BlockSpec((layers, SUB, LANES), lambda i: (0, final, 0)),
            pl.BlockSpec((2, layers, SUB, LANES), lambda i: (0, 0, 0, 0)),
            pl.BlockSpec((2, layers, SUB, LANES), lambda i: (0, 0, final, 0)),
        ],
        out_specs=(out_spec, out_spec),
        compiler_params=params(),
        cost_estimate=pl.CostEstimate(flops=0, bytes_accessed=1 << 20, transcendentals=0),
        name="edge_rows",
    )(layer_depth, layer_depth, momentum, momentum)


def columns_kernel(band_rows, depth_ref, mom_ref, north_ref, south_ref, west_out, east_out):
    lane = lane_index()
    for f, ref in enumerate((depth_ref, mom_ref.at[0], mom_ref.at[1])):
        parts = [jnp.ones((SUB, LANES), jnp.float32)] * 4
        for row in range(-1, band_rows + 1):
            if row < 0:
                x = north_ref[f, 0]
            elif row == band_rows:
                x = south_ref[f, 0]
            else:
                x = ref[pl.ds(row, SUB, stride=band_rows), :]
            if row >= 0:
                x = roll(x, row + 1)
            parts = [
                jnp.where(lane == (row + at) % LANES, x, part)
                for part, at in zip(parts, (1, 2, 0, LANES - 1))
            ]
        west_out[f, 0] = parts[0]
        west_out[f, 1] = roll(parts[1], LANES - 1)
        east_out[f, 0] = roll(parts[2], 1)
        east_out[f, 1] = roll(parts[3], 2)


def edge_columns(depth, mom, north, south, layers):
    band_rows = depth.shape[0] // layers
    block = SUB * band_rows
    halo_spec = pl.BlockSpec((3, 2, SUB, LANES), lambda g: (0, 0, g, 0))
    out = jax.ShapeDtypeStruct((3, 2, layers, LANES), jnp.float32)
    return pl.pallas_call(
        functools.partial(columns_kernel, band_rows),
        grid=(layers // SUB,),
        out_shape=(out, out),
        in_specs=[
            pl.BlockSpec((block, LANES), lambda g: (g, 0)),
            pl.BlockSpec((2, block, LANES), lambda g: (0, g, 0)),
            halo_spec,
            halo_spec,
        ],
        out_specs=(halo_spec, halo_spec),
        compiler_params=params(),
        cost_estimate=pl.CostEstimate(flops=12 * depth.size, bytes_accessed=12 * depth.size, transcendentals=0),
        name="edge_columns",
    )(depth, mom, north, south)


def shortwave_kernel(slots, fresh, absorb_ref, solar_ref, depth_ref, sun_ref, lit_ref, owner_ref, slot_ref, *rest):
    before_ref, heat_out, sent_out, scaled, total = rest[-5:]
    layers, rows, _ = depth_ref.shape
    bands = solar_ref.shape[1]
    sun = sun_ref[...]
    per_sun = -math.log2(math.e) / sun
    for k in range(layers):
        scaled[k] = depth_ref[k] * per_sun
    log_solar = jnp.log2(solar_ref[...])
    top = jnp.zeros((rows, LANES), jnp.float32)
    for first in range(0, bands, SUN_BANDS):
        chunk = range(first, min(first + SUN_BANDS, bands))
        paths = [jnp.broadcast_to(log_solar[:, b : b + 1], (rows, LANES)) for b in chunk]
        for path in paths:
            top = top + jnp.exp2(path)

        def layer(k, paths):
            depth = scaled[k]
            paths = [path + absorb_ref[b, k] * depth for path, b in zip(paths, chunk)]
            downs = [jnp.exp2(path) for path in paths]
            while len(downs) > 1:
                downs = [sum(downs[i : i + 2][1:], downs[i]) for i in range(0, len(downs), 2)]
            total[k] = downs[0] if first == 0 else total[k] + downs[0]
            return paths

        def layers_of(n, paths):
            for i in range(4):
                paths = layer(n * 4 + i, paths)
            return paths

        lax.fori_loop(0, layers // 4, layers_of, paths)
    lit = lit_ref[...] == 1
    lit_lanes = jnp.broadcast_to(lit_ref[...], (rows, LANES)) == 1
    above = top
    for k in range(layers):
        below = total[k]
        absorbed = sun * (above - below)
        heat_out[k] = jnp.where(lit_lanes, absorbed / depth_ref[k], 0.0)
        above = below
    mean = jnp.sum(sun * (top - above), axis=1, keepdims=True) * (1.0 / (layers * LANES))
    target = owner_ref[...] * slots + slot_ref[...]
    target = jnp.broadcast_to(jnp.where(lit, target, -1), (rows, LANES))
    placed = jnp.where(target == lane_index(rows), jnp.broadcast_to(mean, (rows, LANES)), 0.0)
    placed = jnp.sum(placed, axis=0, keepdims=True)

    @pl.when(pl.program_id(0) == 0)
    def _():
        sent_out[...] = placed if fresh else before_ref[...] + placed

    @pl.when(pl.program_id(0) > 0)
    def _():
        sent_out[...] += placed


def shortwave(slots, begin, end, absorption, solar, layer_depth, sun, lit, owner, slot, before, heating):
    layers, band_rows, _ = layer_depth.shape
    fresh = heating is None
    first = begin // SUN_ROWS
    cube = pl.BlockSpec((layers, SUN_ROWS, LANES), lambda i: (0, first + i, 0))
    flat = pl.BlockSpec((SUN_ROWS, LANES), lambda i: (first + i, 0))
    thin = pl.BlockSpec((SUN_ROWS, 1), lambda i: (first + i, 0))
    line = pl.BlockSpec((1, LANES), lambda i: (0, 0))
    operands = [absorption, solar, layer_depth, sun, lit, owner, slot]
    in_specs = [
        pl.BlockSpec(memory_space=pltpu.SMEM),
        pl.BlockSpec(solar.shape, lambda i: (0, 0)),
        cube,
        flat,
        thin,
        thin,
        thin,
    ]
    aliases = {}
    if not fresh:
        aliases = {len(operands): 0}
        operands.append(heating)
        in_specs.append(pl.BlockSpec(memory_space=pl.ANY))
    operands.append(before)
    in_specs.append(line)
    size = layers * (end - begin) * LANES * absorption.shape[0]
    return pl.pallas_call(
        functools.partial(shortwave_kernel, slots, fresh),
        grid=((end - begin) // SUN_ROWS,),
        out_shape=(
            jax.ShapeDtypeStruct(layer_depth.shape, jnp.float32),
            jax.ShapeDtypeStruct((1, LANES), jnp.float32),
        ),
        in_specs=in_specs,
        out_specs=(cube, line),
        scratch_shapes=[pltpu.VMEM((layers, SUN_ROWS, LANES), jnp.float32)] * 2,
        input_output_aliases=aliases,
        compiler_params=params(),
        cost_estimate=pl.CostEstimate(
            flops=4 * size, bytes_accessed=8 * size // absorption.shape[0], transcendentals=size
        ),
        name="shortwave",
    )(*operands)


def ledger_kernel(slots, counts_ref, table_ref, ledger_out):
    sources = table_ref.shape[0]
    here = lax.axis_index("lon")
    lane = lane_index()
    ledger = jnp.zeros((SUB, LANES), jnp.float32)
    start = jnp.int32(0)
    for s in range(sources):
        end = start + counts_ref[0, s]
        values = jnp.broadcast_to(table_ref[s : s + 1, :], (SUB, LANES))
        values = roll(values, lax.rem(start - here * slots + 2 * LANES, LANES))
        ledger = jnp.where((lane >= start) & (lane < end), values, ledger)
        start = end
    ledger_out[...] = ledger[:1, : ledger_out.shape[1]]


def ledger_of(slots, load, counts, table):
    return pl.pallas_call(
        functools.partial(ledger_kernel, slots),
        out_shape=jax.ShapeDtypeStruct((1, load), jnp.float32),
        in_specs=[pl.BlockSpec(memory_space=pltpu.SMEM), pl.BlockSpec(memory_space=pltpu.VMEM)],
        out_specs=pl.BlockSpec(memory_space=pltpu.VMEM),
        compiler_params=params(),
        name="ledger",
    )(counts, table)


def body(
    table,
    layer_depth,
    momentum,
    gravity,
    absorption,
    solar_flux,
    cos_zenith,
    sunlit,
    owner_index,
    slot_index,
    received_counts,
):
    layers, band_rows, width = layer_depth.shape
    lon_parts, lat_parts = lax.axis_size("lon"), lax.axis_size("lat")
    slots = band_rows // lon_parts
    depth = layer_depth.reshape(layers * band_rows, width)
    mom = momentum.reshape(2, layers * band_rows, width)
    solar = solar_flux.reshape(1, -1)

    head, tail = edge_rows(layer_depth, momentum)
    north = lax.ppermute(tail, "lat", [(i, i + 1) for i in range(lat_parts - 1)])
    south = lax.ppermute(head, "lat", [(i + 1, i) for i in range(lat_parts - 1)])

    half = band_rows // 2
    sun_args = (absorption, solar, layer_depth, cos_zenith, sunlit, owner_index, slot_index)
    heating, sent = shortwave(slots, 0, half, *sun_args, jnp.zeros((1, LANES), jnp.float32), None)

    own_west, own_east = edge_columns(depth, mom, north, south, layers)
    west = lax.ppermute(own_east, "lon", [(i, (i + 1) % lon_parts) for i in range(lon_parts)])
    east = lax.ppermute(own_west, "lon", [((i + 1) % lon_parts, i) for i in range(lon_parts)])

    heating, sent = shortwave(slots, half, band_rows, *sun_args, sent, heating)
    arrived = lax.all_gather(sent, "lon", axis=0, tiled=True)

    depth_new, mom_new = dynamics(
        gravity, table, depth, mom, north, south, west, east, own_west, own_east
    )
    ledger = ledger_of(slots, band_rows // 2, received_counts[0], arrived)
    return (
        depth_new.reshape(layer_depth.shape),
        mom_new.reshape(momentum.shape),
        heating,
        ledger[None],
    )


def solution(mesh):
    placed = (
        P(None, "lat", "lon"),
        P(None, None, "lat", "lon"),
        P(),
        P(),
        P(),
        P("lat", "lon"),
        P("lat", "lon"),
        P("lat", "lon"),
        P("lat", "lon"),
        P("lat", "lon", None),
    )

    def whole(layer_depth, *others):
        table = latitude_table(mesh.shape["lat"], layer_depth.shape[1] // mesh.shape["lat"])
        return jax.shard_map(
            functools.partial(body, table),
            mesh=mesh,
            in_specs=placed,
            out_specs=(
                P(None, "lat", "lon"),
                P(None, None, "lat", "lon"),
                P(None, "lat", "lon"),
                P("lat", "lon", None),
            ),
            check_vma=False,
        )(layer_depth, *others)

    return whole
```

time: 372 us -> 77.4 us (0.21)
  the two profiles are of different devices: /device:TPU:1 before, /device:TPU:2 now
where the time goes in v1:
time: 77.4 us; the launch traced here: 77.2 us
  Pallas kernels  42.5 us (55%)
  blocking collectives  18 us (23%)
  starting transfers between devices  10.4 us (13%)
  local copies, waits for them, and re-layouts  3.24 us (4%)
  waiting for transfers between devices  2.2 us (3%)
  between operations  0.78 us (1%)
    pallas_call x1, Pallas kernels, dynamics(): pl.pallas_call(functools.partial(dynamics_kernel, band_rows), grid=(layer...  22.1 us
    all_gather x1, blocking collectives, body(): arrived = lax.all_gather(sent, 'lon', axis=0, tiled=True)  18 us
    pallas_call x2, Pallas kernels, shortwave(): pl.pallas_call(functools.partial(shortwave_kernel, slots, fresh), grid=((...  16.5 us
    ppermute x1, starting transfers between devices, body(): lax.ppermute(head, 'lat', [(i + 1, i) for i in range(lat_parts - 1)])  3.64 us
    unnamed x30, local copies, waits for them, and re-layouts  3.23 us
    ppermute x1, starting transfers between devices, body(): lax.ppermute(own_west, 'lon', [((i + 1) % lon_parts, i) for i in range(lo...  3.2 us
    pallas_call x1, Pallas kernels, edge_columns(): pl.pallas_call(functools.partial(columns_kernel, band_rows), grid=(layers...  2.68 us
    ppermute x1, starting transfers between devices, body(): lax.ppermute(tail, 'lat', [(i, i + 1) for i in range(lat_parts - 1)])  2.05 us
  transfers between devices with their start and end apart: 4, of which 2 were waited for; matrix products, arithmetic and copies ran while one was open for 0% of the time, Pallas kernels for 23%

profile of v1, /device:TPU:2, one launch (start us, length us, event | category | flops | bytes accessed | tf_op | source)
XLA Modules:
  0.0 77.2 jit_solution(2434923890624080596)
XLA Ops:
  0.6 0.0 copy-start
  0.6 1.6 %copy-done = f32[2,32,64,128]{3,2,1,0:T(8,128)S(1)} copy-done((f32[2,32,64,128]{3,2,1,0:T(8,128)S(1)}, f32[2,32,64,128]{3,2,1,0:T(8,128)}, u32[]{:S(2)}) %copy-start) | copy-done | bytes 2097176
  2.2 1.2 %copy-done.2 = f32[32,64,128]{2,1,0:T(8,128)S(1)} copy-done((f32[32,64,128]{2,1,0:T(8,128)S(1)}, f32[32,64,128]{2,1,0:T(8,128)}, u32[]{:S(2)}) %copy-start.2) | copy-done | bytes 1048600
  3.4 0.1 edge_rows.1
  3.6 0.0 copy-start.11
  3.6 0.0 copy-start.12
  3.6 0.0 copy-start.5
  3.6 0.0 copy-start.6
  3.6 2.1 %collective-permute-start = (f32[3,2,32,128]{3,2,1,0:T(8,128)S(1)}, f32[3,2,32,128]{3,2,1,0:T(8,128)S(1)}, u32[]{:S(2)}, u32[]{:S(2)}) collective-permute-start(f32[3,2,32,128]{3,2,1,0:T(8,128)S(1)} %get-tuple-element.14), channel_id=1, source_target_pairs={{0,1},{1,2},{2,3},{4,5},{5,6},{6,7},{8,9},{9,10},{10,11},{12,13},{... | collective-permute-start | bytes 294920 | tf_op jit(solution)/shard_map/ppermute | solution.py:525
  5.7 3.6 %collective-permute-start.1 = (f32[3,2,32,128]{3,2,1,0:T(8,128)S(1)}, f32[3,2,32,128]{3,2,1,0:T(8,128)S(1)}, u32[]{:S(2)}, u32[]{:S(2)}) collective-permute-start(f32[3,2,32,128]{3,2,1,0:T(8,128)S(1)} %get-tuple-element.15), channel_id=1, source_target_pairs={{1,0},{2,1},{3,2},{5,4},{6,5},{7,6},{9,8},{10,9},{11,10},{13,12},{... | collective-permute-start | bytes 294920 | tf_op jit(solution)/shard_map/ppermute | solution.py:526
  9.3 0.4 collective-permute-done.north_ref
  9.7 1.8 %collective-permute-done.1.south_ref = f32[3,2,32,128]{3,2,1,0:T(8,128)S(1)} collective-permute-done((f32[3,2,32,128]{3,2,1,0:T(8,128)S(1)}, f32[3,2,32,128]{3,2,1,0:T(8,128)S(1)}, u32[]{:S(2)}, u32[]{:S(2)}) %collective-permute-start.1) | collective-permute-done | bytes 98336 | tf_op jit(solution)/shard_map/ppermute | solution.py:526
  11.5 2.7 %edge_columns.1 = (f32[3,2,32,128]{3,2,1,0:T(8,128)S(1)}, f32[3,2,32,128]{3,2,1,0:T(8,128)S(1)}) custom-call(f32[2048,128]{1,0:T(8,128)S(1)} %bitcast.11, f32[2,2048,128]{2,1,0:T(8,128)S(1)} %bitcast.9, f32[3,2,32,128]{3,2,1,0:T(8,128)S(1)} %collective-permute-done.north_ref, f32[3,2,32,128]{3,2,1,0:T(8,128)S(1)} %collective-permute-done.1.south_ref), custom_call_target="tpu_custom_call" | custom-call | flops 3145728 | bytes 3145728 | tf_op jit(solution)/shard_map/edge_columns/pallas_call | solution.py:362
  14.2 1.5 %collective-permute-start.2 = (f32[3,2,32,128]{3,2,1,0:T(8,128)S(1)}, f32[3,2,32,128]{3,2,1,0:T(8,128)S(1)}, u32[]{:S(2)}, u32[]{:S(2)}) collective-permute-start(f32[3,2,32,128]{3,2,1,0:T(8,128)S(1)} %get-tuple-element.16.own_east_ref), channel_id=1, source_target_pairs={{0,4},{4,8},{8,12},{12,16},{16,20},{20,24},{24,28},{28,0},{1,5},{5... | collective-permute-start | bytes 294920 | tf_op jit(solution)/shard_map/ppermute | solution.py:533
  15.8 3.2 %collective-permute-start.3 = (f32[3,2,32,128]{3,2,1,0:T(8,128)S(1)}, f32[3,2,32,128]{3,2,1,0:T(8,128)S(1)}, u32[]{:S(2)}, u32[]{:S(2)}) collective-permute-start(f32[3,2,32,128]{3,2,1,0:T(8,128)S(1)} %get-tuple-element.17.own_west_ref), channel_id=1, source_target_pairs={{4,0},{8,4},{12,8},{16,12},{20,16},{24,20},{28,24},{0,28},{5,1},{9... | collective-permute-start | bytes 294920 | tf_op jit(solution)/shard_map/ppermute | solution.py:534
  19.0 0.1 copy.29.absorb_ref
  19.1 0.1 copy.30.lit_ref
  19.2 0.1 copy.31.owner_ref
  19.3 0.1 copy.32.slot_ref
  19.4 8.2 %shortwave.2 = (f32[32,64,128]{2,1,0:T(8,128)}, f32[1,128]{1,0:T(1,128)S(1)}) custom-call(f32[56,32]{1,0:T(8,128)S(1)} %copy.29.absorb_ref, f32[1,56]{1,0:T(1,128)S(1)} %bitcast.16, f32[32,64,128]{2,1,0:T(8,128)S(1)} %copy-done.3, f32[64,128]{1,0:T(8,128)S(1)} %copy-done.5, s32[64,1]{1,0:T(8,128)S(1)} %copy.30.lit_ref, s32[64,1]{1,0:T(8,128)S(1)} %copy.31.owner_ref, ...), custom_call_target="tpu_custom_call" | custom-call | flops 29360128 | bytes 1048576 | tf_op jit(solution)/shard_map/shortwave/pallas_call | solution.py:459
  27.6 8.3 %shortwave.3 = (f32[32,64,128]{2,1,0:T(8,128)}, f32[1,128]{1,0:T(1,128)S(1)}) custom-call(f32[56,32]{1,0:T(8,128)S(1)} %copy.29.absorb_ref, f32[1,56]{1,0:T(1,128)S(1)} %bitcast.17, f32[32,64,128]{2,1,0:T(8,128)S(1)} %copy-done.3, f32[64,128]{1,0:T(8,128)S(1)} %copy-done.5, s32[64,1]{1,0:T(8,128)S(1)} %copy.30.lit_ref, ...), custom_call_target="tpu_custom_call", output_to_operand_aliasing={{0}: (7, {})} | custom-call | flops 29360128 | bytes 1048576 | tf_op jit(solution)/shard_map/shortwave/pallas_call | solution.py:459
  35.9 18.0 %all-gather = f32[8,1,128]{2,1,0:T(1,128)S(1)} all-gather(f32[1,1,128]{2,1,0:T(1,128)S(1)} %bitcast.15), channel_id=1, replica_groups=mesh['lon'=8,'lat'=4] {'lon'}, dimensions={0}, use_global_device_ids=true | all-gather | bytes 4608 | tf_op jit(solution)/shard_map/all_gather | solution.py:537
  53.9 1.1 %ledger.1 = f32[1,32]{1,0:T(1,128)} custom-call(s32[1,8]{1,0:T(1,128)S(1)} %bitcast.14, f32[8,128]{1,0:T(8,128)S(1)} %bitcast.13), custom_call_target="tpu_custom_call" | custom-call | tf_op jit(solution)/shard_map/ledger/pallas_call | solution.py:494
  55.1 22.1 %dynamics.1 = (f32[2048,128]{1,0:T(8,128)}, f32[2,2048,128]{2,1,0:T(8,128)}) custom-call(f32[32]{0:T(128)S(1)} %copy-done.7, f32[32,128]{1,0:T(8,128)S(1)} %copy-done.8, f32[32,128]{1,0:T(8,128)S(1)} %copy-done.8, f32[2048,128]{1,0:T(8,128)S(1)} %bitcast.12, f32[2,2048,128]{2,1,0:T(8,128)S(1)} %bitcast.10, ...), custom_call_target="tpu_custom_call" | custom-call | flops 57671680 | bytes 6291456 | tf_op jit(solution)/shard_map/dynamics/pallas_call | solution.py:270
  (22 shorter events, 0.1 us)
Async XLA Ops:
  0.6 1.6 %copy-start = (f32[2,32,64,128]{3,2,1,0:T(8,128)S(1)}, f32[2,32,64,128]{3,2,1,0:T(8,128)}, u32[]{:S(2)}) copy-start(f32[2,32,64,128]{3,2,1,0:T(8,128)} %mom_tail.1) | copy-start | bytes 6291460
  2.2 1.2 %copy-start.2 = (f32[32,64,128]{2,1,0:T(8,128)S(1)}, f32[32,64,128]{2,1,0:T(8,128)}, u32[]{:S(2)}) copy-start(f32[32,64,128]{2,1,0:T(8,128)} %depth_ref.3) | copy-start | bytes 3145732
  3.6 15.4 %copy-start.9 = (f32[56,32]{0,1:T(8,128)S(1)}, f32[56,32]{0,1:T(8,128)}, u32[]{:S(2)}) copy-start(f32[56,32]{0,1:T(8,128)} %param.14) | copy-start | bytes 21508
  3.6 15.5 %copy-start.10 = (s32[64,1]{0,1:T(1,128)S(1)}, s32[64,1]{0,1:T(1,128)}, u32[]{:S(2)}) copy-start(s32[64,1]{0,1:T(1,128)} %param.17) | copy-start | bytes 772
  3.6 15.6 %copy-start.11 = (s32[64,1]{0,1:T(1,128)S(1)}, s32[64,1]{0,1:T(1,128)}, u32[]{:S(2)}) copy-start(s32[64,1]{0,1:T(1,128)} %param.18) | copy-start | bytes 772
  3.6 15.7 %copy-start.12 = (s32[64,1]{0,1:T(1,128)S(1)}, s32[64,1]{0,1:T(1,128)}, u32[]{:S(2)}) copy-start(s32[64,1]{0,1:T(1,128)} %param.19) | copy-start | bytes 772
  3.6 15.8 %copy-start.3 = (f32[32,64,128]{2,1,0:T(8,128)S(1)}, f32[32,64,128]{2,1,0:T(8,128)}, u32[]{:S(2)}) copy-start(f32[32,64,128]{2,1,0:T(8,128)} %depth_ref.3) | copy-start | bytes 3145732
  3.6 15.8 %copy-start.5 = (f32[64,128]{1,0:T(8,128)S(1)}, f32[64,128]{1,0:T(8,128)}, u32[]{:S(2)}) copy-start(f32[64,128]{1,0:T(8,128)} %sun_ref.3) | copy-start | bytes 98308
  3.6 15.8 %copy-start.6 = (f32[56]{0:T(128)S(1)}, f32[56]{0:T(128)}, u32[]{:S(2)}) copy-start(f32[56]{0:T(128)} %param.15) | copy-start | bytes 676
  3.6 6.1 %collective-permute-start = (f32[3,2,32,128]{3,2,1,0:T(8,128)S(1)}, f32[3,2,32,128]{3,2,1,0:T(8,128)S(1)}, u32[]{:S(2)}, u32[]{:S(2)}) collective-permute-start(f32[3,2,32,128]{3,2,1,0:T(8,128)S(1)} %get-tuple-element.14), channel_id=1, source_target_pairs={{0,1},{1,2},{2,3},{4,5},{5,6},{6,7},{8,9},{9,10},{10,11},{12,13},{... | collective-permute-start | bytes 294920 | tf_op jit(solution)/shard_map/ppermute | solution.py:525
  5.7 5.8 %collective-permute-start.1 = (f32[3,2,32,128]{3,2,1,0:T(8,128)S(1)}, f32[3,2,32,128]{3,2,1,0:T(8,128)S(1)}, u32[]{:S(2)}, u32[]{:S(2)}) collective-permute-start(f32[3,2,32,128]{3,2,1,0:T(8,128)S(1)} %get-tuple-element.15), channel_id=1, source_target_pairs={{1,0},{2,1},{3,2},{5,4},{6,5},{7,6},{9,8},{10,9},{11,10},{13,12},{... | collective-permute-start | bytes 294920 | tf_op jit(solution)/shard_map/ppermute | solution.py:526
  14.2 40.8 %collective-permute-start.2 = (f32[3,2,32,128]{3,2,1,0:T(8,128)S(1)}, f32[3,2,32,128]{3,2,1,0:T(8,128)S(1)}, u32[]{:S(2)}, u32[]{:S(2)}) collective-permute-start(f32[3,2,32,128]{3,2,1,0:T(8,128)S(1)} %get-tuple-element.16.own_east_ref), channel_id=1, source_target_pairs={{0,4},{4,8},{8,12},{12,16},{16,20},{20,24},{24,28},{28,0},{1,5},{5... | collective-permute-start | bytes 294920 | tf_op jit(solution)/shard_map/ppermute | solution.py:533
  15.8 39.3 %collective-permute-start.3 = (f32[3,2,32,128]{3,2,1,0:T(8,128)S(1)}, f32[3,2,32,128]{3,2,1,0:T(8,128)S(1)}, u32[]{:S(2)}, u32[]{:S(2)}) collective-permute-start(f32[3,2,32,128]{3,2,1,0:T(8,128)S(1)} %get-tuple-element.17.own_west_ref), channel_id=1, source_target_pairs={{4,0},{8,4},{12,8},{16,12},{20,16},{24,20},{28,24},{0,28},{5,1},{9... | collective-permute-start | bytes 294920 | tf_op jit(solution)/shard_map/ppermute | solution.py:534
  27.6 26.3 %copy-start.4 = (s32[1,1,8]{2,1,0:T(1,128)S(1)}, s32[1,1,8]{2,1,0:T(1,128)}, u32[]{:S(2)}) copy-start(s32[1,1,8]{2,1,0:T(1,128)} %param.20) | copy-start | bytes 100
  27.6 27.4 %copy-start.1 = (f32[2,32,64,128]{3,2,1,0:T(8,128)S(1)}, f32[2,32,64,128]{3,2,1,0:T(8,128)}, u32[]{:S(2)}) copy-start(f32[2,32,64,128]{3,2,1,0:T(8,128)} %mom_tail.1) | copy-start | bytes 6291460
  27.6 27.4 %copy-start.7 = (f32[32]{0:T(128)S(1)}, f32[32]{0:T(128)}, u32[]{:S(2)}) copy-start(f32[32]{0:T(128)} %gravity_ref.1) | copy-start | bytes 388
  27.6 27.4 %copy-start.8 = (f32[32,128]{1,0:T(8,128)S(1)}, f32[32,128]{1,0:T(8,128)}, u32[]{:S(2)}) copy-start(f32[32,128]{1,0:T(8,128)} %constant.4.clone.table_ref.lanes_ref) | copy-start | bytes 49156

commit v2 on v1

--- a/solution.py
+++ b/solution.py
@@ -15,13 +15,16 @@
 LAT_SPAN = 0.62
 LANES = 128
 SUB = 8
-SUN_ROWS = 16
-SUN_BANDS = 14
-VMEM_LIMIT = 48 * 1024 * 1024
-
-
-def params(**more):
-    return pltpu.CompilerParams(vmem_limit_bytes=VMEM_LIMIT, **more)
+SUN_ROWS = 32
+SUN_BANDS = 7
+SUN_LAYERS = 8
+DEEP = 16
+BLOCK_ROWS = 6
+MIB = 1024 * 1024
+
+
+def params(limit=24):
+    return pltpu.CompilerParams(vmem_limit_bytes=limit * MIB)
 
 
 def lane_index(rows=SUB):
@@ -107,20 +110,28 @@
     own_east_ref,
     depth_out,
     mom_out,
-    middle,
+    first_state,
+    middle_state,
+    shifted,
+    partial,
+    east_fluxes,
+    edge_fluxes,
 ):
+    deep = depth_ref.shape[0] // band_rows
     group = pl.program_id(0)
     lat = lax.axis_index("lat")
     at_first = lat == 0
     at_final = lat == lax.axis_size("lat") - 1
-    lane = lane_index()
-    sublane = lax.broadcasted_iota(jnp.int32, (SUB, LANES), 0)
-    gravity = jnp.zeros((SUB, LANES), jnp.float32)
-    for i in range(SUB):
-        gravity = jnp.where(sublane == i, gravity_ref[group * SUB + i], gravity)
+    layer = lax.broadcasted_iota(jnp.int32, (deep, LANES), 0)
+    gravity = jnp.zeros((deep, LANES), jnp.float32)
+    for i in range(deep):
+        gravity = jnp.where(layer == i, gravity_ref[group * deep + i], gravity)
+    lane = lane_index(deep)
+    is_first_lane = lane == 0
+    is_last_lane = lane == LANES - 1
 
     both = jnp.concatenate([gravity, gravity], axis=0)
-    lane2 = lane_index(2 * SUB)
+    lane2 = lane_index(2 * deep)
     low_edge = (lane2 == 0) & at_first
     high_edge = (lane2 == band_rows + 1) & at_final
 
@@ -139,7 +150,7 @@
         column(lambda f: own_west_ref[f, 1], lambda f: east_ref[f, 1]),
     ]
     rate_of, upper_cos, lower_cos, turn_of = (
-        jnp.broadcast_to(lanes_ref[pl.ds(lat * 8 + q, 1), :], (2 * SUB, LANES)) for q in range(4)
+        jnp.broadcast_to(lanes_ref[pl.ds(lat * 8 + q, 1), :], (2 * deep, LANES)) for q in range(4)
     )
     fluxes = [face(east_side(a), east_side(b)) for a, b in zip(columns[:-1], columns[1:])]
     moved = []
@@ -153,130 +164,176 @@
             for i in range(3)
         )
         moved.append(cell(*turned(c[:3], change, rate_of, turn_of), both))
-    edge_fluxes = (fluxes[1], face(east_side(moved[0]), east_side(moved[1])))
-
-    is_first_lane = lane == 0
-    is_last_lane = lane == LANES - 1
-
-    def advance_row(row, here, above, below_flux, edges):
+    for step, edges in enumerate((fluxes[1], face(east_side(moved[0]), east_side(moved[1])))):
+        for i in range(3):
+            edge_fluxes[step, i] = edges[i]
+
+    def at(index):
+        start = index * deep
+        return pl.ds(start if isinstance(start, int) else pl.multiple_of(start, SUB), deep)
+
+    def store(ref, index, values):
+        for f in range(3):
+            ref[f, at(index), :] = values[f]
+
+    def fetch(ref, index):
+        return tuple(ref[f, at(index), :] for f in range(3))
+
+    def inside(row):
+        window = pl.ds(row, deep, stride=band_rows)
+        return depth_ref[window, :], mom_ref.at[0][window, :], mom_ref.at[1][window, :]
+
+    def outer(ref, which, clamped, edge_row):
+        here = inside(edge_row)
+        return tuple(jnp.where(clamped, here[f], ref[f, which]) for f in range(3))
+
+    def rotate(row, raw):
+        store(shifted, row + 1, tuple(roll(x, 1) for x in raw))
+
+    def faces(state, offset, row, here, below):
+        above = cell(*fetch(state, row + 1 + offset), gravity)
+        upper = face(north_side(here), north_side(above))
+        cos_upper = table_ref[lat * 8 + 1, row + 1]
+        upper = (cos_upper * upper[0], cos_upper * upper[2], cos_upper * upper[1])
+        rate = table_ref[lat * 8, row + 1]
+        store(partial, row + 1, tuple(here[i] - rate * (upper[i] - below[i]) for i in range(3)))
+        west = cell(*fetch(shifted, row + 1), gravity)
+        store(east_fluxes, row + 1, face(east_side(west), east_side(here)))
+        return above, upper
+
+    def update(step, row):
         j = row + 1
         rate = table_ref[lat * 8, j]
-        cos_upper = table_ref[lat * 8 + 1, j]
         turning = table_ref[lat * 8 + 3, j]
-        upper = face(north_side(here), north_side(above))
-        upper = (cos_upper * upper[0], cos_upper * upper[2], cos_upper * upper[1])
-        side = east_side(here)
-        flux = face(tuple(roll(x, 1) for x in side), side)
-        change = []
+        state = []
         for i in range(3):
-            west_edge = roll(edges[i][:SUB], lax.rem(2 * LANES - j, LANES))
-            east_edge = roll(edges[i][SUB:], lax.rem(2 * LANES - 1 - j, LANES))
-            west_flux = jnp.where(is_first_lane, west_edge, flux[i])
-            east_flux = jnp.where(is_last_lane, east_edge, roll(flux[i], LANES - 1))
-            change.append((east_flux - west_flux) + (upper[i] - below_flux[i]))
-        return turned(here[:3], change, rate, turning), upper
-
-    def weighted(row, below, here):
+            flux = east_fluxes[i, at(j), :]
+            west_edge = roll(edge_fluxes[step, i, pl.ds(0, deep), :], lax.rem(2 * LANES - j, LANES))
+            east_edge = roll(edge_fluxes[step, i, pl.ds(deep, deep), :], lax.rem(2 * LANES - 1 - j, LANES))
+            west_flux = jnp.where(is_first_lane, west_edge, flux)
+            east_flux = jnp.where(is_last_lane, east_edge, roll(flux, LANES - 1))
+            state.append(partial[i, at(j), :] - rate * (east_flux - west_flux))
+        depth, east_mom, north_mom = state
+        return depth, east_mom + turning * north_mom, north_mom - turning * east_mom
+
+    def start(state, offset, row):
+        below = cell(*fetch(state, row - 1 + offset), gravity)
+        here = cell(*fetch(state, row + offset), gravity)
+        flux = face(north_side(below), north_side(here))
         cos_lower = table_ref[lat * 8 + 2, row + 1]
-        flux = face(north_side(below), north_side(here))
-        return cos_lower * flux[0], cos_lower * flux[2], cos_lower * flux[1]
-
-    def block_row(row):
-        window = pl.ds(row, SUB, stride=band_rows)
-        return cell(depth_ref[window, :], mom_ref.at[0][window, :], mom_ref.at[1][window, :], gravity)
-
-    def halo_row(ref, which, clamped, edge_row):
-        window = pl.ds(edge_row, SUB, stride=band_rows)
-        inside = (depth_ref[window, :], mom_ref.at[0][window, :], mom_ref.at[1][window, :])
-        return cell(*(jnp.where(clamped, inside[f], ref[f, which]) for f in range(3)), gravity)
-
-    def store_middle(row, state):
-        for f in range(3):
-            middle[f, pl.ds(pl.multiple_of((row + 1) * SUB, SUB), SUB), :] = state[f]
-
-    def middle_row(row):
-        window = pl.ds(pl.multiple_of((row + 1) * SUB, SUB), SUB)
-        return cell(*(middle[f, window, :] for f in range(3)), gravity)
-
-    edges = edge_fluxes[0]
-    below, here = (halo_row(north_ref, which, at_first, 0) for which in (1, 0))
-    flux = weighted(-1, below, here)
-    above = block_row(0)
-    state, flux = advance_row(-1, here, above, flux, edges)
-    store_middle(-1, state)
-
-    def first_step(unroll):
-        def rows(n, carry):
-            here, flux = carry
-            for i in range(unroll):
-                row = n * unroll + i
-                above = block_row(row + 1)
-                state, flux = advance_row(row, here, above, flux, edges)
-                store_middle(row, state)
-                here = above
-            return here, flux
-
-        return rows
-
-    unroll = 7 if (band_rows - 1) % 7 == 0 else 1
-    here, flux = lax.fori_loop(0, (band_rows - 1) // unroll, first_step(unroll), (above, flux))
-    for row, above in (
-        (band_rows - 1, halo_row(south_ref, 0, at_final, band_rows - 1)),
-        (band_rows, halo_row(south_ref, 1, at_final, band_rows - 1)),
+        return here, (cos_lower * flux[0], cos_lower * flux[2], cos_lower * flux[1])
+
+    def walk(first_row, rows, prepare, middle, finish):
+        blocks, left = divmod(rows, BLOCK_ROWS)
+
+        def span(n):
+            return [first_row + n * BLOCK_ROWS + i for i in range(BLOCK_ROWS)]
+
+        def each(f, n):
+            for row in span(n):
+                f(row)
+
+        def middle_rows(rows_of, carry):
+            for row in rows_of:
+                carry = middle(row, carry)
+            return carry
+
+        each(prepare, 0)
+        each(prepare, 1)
+        carry = middle_rows(span(0), None)
+
+        def full(n, carry):
+            each(finish, n - 1)
+            carry = middle_rows(span(n), carry)
+            each(prepare, n + 1)
+            return carry
+
+        carry = lax.fori_loop(1, blocks - 1, full, carry)
+        tail = [first_row + blocks * BLOCK_ROWS + i for i in range(left)]
+        each(finish, blocks - 2)
+        carry = middle_rows(span(blocks - 1), carry)
+        for row in tail:
+            prepare(row)
+        each(finish, blocks - 1)
+        middle_rows(tail, carry)
+        for row in tail:
+            finish(row)
+
+    for row, ref, which, clamped, edge_row in (
+        (-2, north_ref, 1, at_first, 0),
+        (-1, north_ref, 0, at_first, 0),
+        (band_rows, south_ref, 0, at_final, band_rows - 1),
+        (band_rows + 1, south_ref, 1, at_final, band_rows - 1),
     ):
-        state, flux = advance_row(row, here, above, flux, edges)
-        store_middle(row, state)
-        here = above
+        raw = outer(ref, which, clamped, edge_row)
+        store(first_state, row + 2, raw)
+        if -1 <= row <= band_rows:
+            rotate(row, raw)
+
+    def prepare1(row):
+        ahead = jnp.minimum(row + 1, band_rows - 1)
+        raw = inside(ahead)
+        store(first_state, ahead + 2, raw)
+        rotate(ahead, raw)
+
+    def middle1(row, carry):
+        if carry is None:
+            carry = start(first_state, 2, row)
+        return faces(first_state, 2, row, *carry)
+
+    def finish1(row):
+        store(middle_state, row + 1, update(0, row))
+
+    walk(-1, band_rows + 2, prepare1, middle1, finish1)
 
     @pl.when(at_first)
     def _():
-        for f in range(3):
-            middle[f, pl.ds(0, SUB), :] = middle[f, pl.ds(SUB, SUB), :]
+        store(middle_state, 0, fetch(middle_state, 1))
 
     @pl.when(at_final)
     def _():
-        for f in range(3):
-            middle[f, pl.ds((band_rows + 1) * SUB, SUB), :] = middle[f, pl.ds(band_rows * SUB, SUB), :]
-
-    edges2 = edge_fluxes[1]
-    here = middle_row(0)
-    flux = weighted(0, middle_row(-1), here)
-    unroll2 = 8 if band_rows % 8 == 0 else 1
-
-    def second_step(n, carry):
-        here, flux = carry
-        for i in range(unroll2):
-            row = n * unroll2 + i
-            above = middle_row(row + 1)
-            state, flux = advance_row(row, here, above, flux, edges2)
-            window = pl.ds(row, SUB, stride=band_rows)
-            depth_out[window, :] = state[0]
-            mom_out.at[0][window, :] = state[1]
-            mom_out.at[1][window, :] = state[2]
-            here = above
-        return here, flux
-
-    lax.fori_loop(0, band_rows // unroll2, second_step, (here, flux))
+        store(middle_state, band_rows + 1, fetch(middle_state, band_rows))
+
+    def prepare2(row):
+        rotate(row, fetch(middle_state, row + 1))
+
+    def middle2(row, carry):
+        if carry is None:
+            carry = start(middle_state, 1, row)
+        return faces(middle_state, 1, row, *carry)
+
+    def finish2(row):
+        window = pl.ds(row, deep, stride=band_rows)
+        state = update(1, row)
+        depth_out[window, :] = state[0]
+        mom_out.at[0][window, :] = state[1]
+        mom_out.at[1][window, :] = state[2]
+
+    walk(0, band_rows, prepare2, middle2, finish2)
 
 
 def dynamics(gravity, table, depth, mom, north, south, west, east, own_west, own_east):
     layers, band_rows = gravity.shape[0], depth.shape[0] // gravity.shape[0]
-    block = SUB * band_rows
+    deep = DEEP
+    block = deep * band_rows
     smem = pl.BlockSpec(memory_space=pltpu.SMEM)
     whole = pl.BlockSpec(table.shape, lambda g: (0, 0))
     depth_spec = pl.BlockSpec((block, LANES), lambda g: (g, 0))
     mom_spec = pl.BlockSpec((2, block, LANES), lambda g: (0, g, 0))
-    halo_spec = pl.BlockSpec((3, 2, SUB, LANES), lambda g: (0, 0, g, 0))
+    halo_spec = pl.BlockSpec((3, 2, deep, LANES), lambda g: (0, 0, g, 0))
+    rows_of = lambda rows: pltpu.VMEM((3, rows * deep, LANES), jnp.float32)
     return pl.pallas_call(
         functools.partial(dynamics_kernel, band_rows),
-        grid=(layers // SUB,),
+        grid=(layers // deep,),
         out_shape=(
             jax.ShapeDtypeStruct(depth.shape, jnp.float32),
             jax.ShapeDtypeStruct(mom.shape, jnp.float32),
         ),
         in_specs=[smem, smem, whole, depth_spec, mom_spec] + [halo_spec] * 6,
         out_specs=(depth_spec, mom_spec),
-        scratch_shapes=[pltpu.VMEM((3, (band_rows + 2) * SUB, LANES), jnp.float32)],
+        scratch_shapes=[rows_of(band_rows + 4)]
+        + [rows_of(band_rows + 2)] * 4
+        + [pltpu.VMEM((2, 3, 2 * deep, LANES), jnp.float32)],
         compiler_params=params(),
         cost_estimate=pl.CostEstimate(
             flops=220 * depth.size, bytes_accessed=24 * depth.size, transcendentals=8 * depth.size
@@ -325,7 +382,7 @@
             pl.BlockSpec((2, layers, SUB, LANES), lambda i: (0, 0, final, 0)),
         ],
         out_specs=(out_spec, out_spec),
-        compiler_params=params(),
+        compiler_params=params(60),
         cost_estimate=pl.CostEstimate(flops=0, bytes_accessed=1 << 20, transcendentals=0),
         name="edge_rows",
     )(layer_depth, layer_depth, momentum, momentum)
@@ -376,8 +433,8 @@
     )(depth, mom, north, south)
 
 
-def shortwave_kernel(slots, fresh, absorb_ref, solar_ref, depth_ref, sun_ref, lit_ref, owner_ref, slot_ref, *rest):
-    before_ref, heat_out, sent_out, scaled, total = rest[-5:]
+def shortwave_kernel(slots, first, fresh, absorb_ref, solar_ref, depth_ref, sun_ref, lit_ref, owner_ref, slot_ref, *rest):
+    heat_out, sent_out, scaled, total = rest[-4:]
     layers, rows, _ = depth_ref.shape
     bands = solar_ref.shape[1]
     sun = sun_ref[...]
@@ -386,29 +443,36 @@
         scaled[k] = depth_ref[k] * per_sun
     log_solar = jnp.log2(solar_ref[...])
     top = jnp.zeros((rows, LANES), jnp.float32)
-    for first in range(0, bands, SUN_BANDS):
-        chunk = range(first, min(first + SUN_BANDS, bands))
+    for begin in range(0, bands, SUN_BANDS):
+        chunk = range(begin, min(begin + SUN_BANDS, bands))
         paths = [jnp.broadcast_to(log_solar[:, b : b + 1], (rows, LANES)) for b in chunk]
         for path in paths:
             top = top + jnp.exp2(path)
 
         def layer(k, paths):
             depth = scaled[k]
-            paths = [path + absorb_ref[b, k] * depth for path, b in zip(paths, chunk)]
-            downs = [jnp.exp2(path) for path in paths]
-            while len(downs) > 1:
-                downs = [sum(downs[i : i + 2][1:], downs[i]) for i in range(0, len(downs), 2)]
-            total[k] = downs[0] if first == 0 else total[k] + downs[0]
+            paths = [path + absorb_ref[k, b] * depth for path, b in zip(paths, chunk)]
+            downs = [None, None]
+            for i, path in enumerate(paths):
+                down = jnp.exp2(path)
+                downs[i % 2] = down if downs[i % 2] is None else downs[i % 2] + down
+            downs = [sum(downs[1:], downs[0])]
+            total[k] = downs[0] if begin == 0 else total[k] + downs[0]
             return paths
 
         def layers_of(n, paths):
-            for i in range(4):
-                paths = layer(n * 4 + i, paths)
+            for i in range(SUN_LAYERS):
+                paths = layer(n * SUN_LAYERS + i, paths)
             return paths
 
-        lax.fori_loop(0, layers // 4, layers_of, paths)
-    lit = lit_ref[...] == 1
-    lit_lanes = jnp.broadcast_to(lit_ref[...], (rows, LANES)) == 1
+        lax.fori_loop(0, layers // SUN_LAYERS, layers_of, paths)
+    place = jnp.where(lit_ref[...] == 1, owner_ref[...] * slots + slot_ref[...], -1).astype(jnp.float32)
+    band_rows = place.shape[1]
+    row = (first + pl.program_id(0)) * rows + lax.broadcasted_iota(jnp.int32, (rows, band_rows), 0)
+    own = row == lax.broadcasted_iota(jnp.int32, (rows, band_rows), 1)
+    place = jnp.sum(jnp.where(own, jnp.broadcast_to(place, own.shape), 0.0), axis=1, keepdims=True)
+    place = jnp.broadcast_to(place, (rows, LANES))
+    lit_lanes = place >= 0.0
     above = top
     for k in range(layers):
         below = total[k]
@@ -416,14 +480,14 @@
         heat_out[k] = jnp.where(lit_lanes, absorbed / depth_ref[k], 0.0)
         above = below
     mean = jnp.sum(sun * (top - above), axis=1, keepdims=True) * (1.0 / (layers * LANES))
-    target = owner_ref[...] * slots + slot_ref[...]
-    target = jnp.broadcast_to(jnp.where(lit, target, -1), (rows, LANES))
-    placed = jnp.where(target == lane_index(rows), jnp.broadcast_to(mean, (rows, LANES)), 0.0)
-    placed = jnp.sum(placed, axis=0, keepdims=True)
+    placed = jnp.where(
+        place == lane_index(rows).astype(jnp.float32), jnp.broadcast_to(mean, (rows, LANES)), 0.0
+    )
+    placed = jnp.broadcast_to(jnp.sum(placed, axis=0, keepdims=True), sent_out.shape)
 
     @pl.when(pl.program_id(0) == 0)
     def _():
-        sent_out[...] = placed if fresh else before_ref[...] + placed
+        sent_out[...] = placed if fresh else rest[1][...] + placed
 
     @pl.when(pl.program_id(0) > 0)
     def _():
@@ -436,8 +500,9 @@
     first = begin // SUN_ROWS
     cube = pl.BlockSpec((layers, SUN_ROWS, LANES), lambda i: (0, first + i, 0))
     flat = pl.BlockSpec((SUN_ROWS, LANES), lambda i: (first + i, 0))
-    thin = pl.BlockSpec((SUN_ROWS, 1), lambda i: (first + i, 0))
-    line = pl.BlockSpec((1, LANES), lambda i: (0, 0))
+    thin = pl.BlockSpec((1, band_rows), lambda i: (0, 0))
+    parts = band_rows // slots
+    line = pl.BlockSpec((parts, LANES), lambda i: (0, 0))
     operands = [absorption, solar, layer_depth, sun, lit, owner, slot]
     in_specs = [
         pl.BlockSpec(memory_space=pltpu.SMEM),
@@ -453,15 +518,15 @@
         aliases = {len(operands): 0}
         operands.append(heating)
         in_specs.append(pl.BlockSpec(memory_space=pl.ANY))
-    operands.append(before)
-    in_specs.append(line)
-    size = layers * (end - begin) * LANES * absorption.shape[0]
+        operands.append(before)
+        in_specs.append(line)
+    size = layers * (end - begin) * LANES * absorption.shape[1]
     return pl.pallas_call(
-        functools.partial(shortwave_kernel, slots, fresh),
+        functools.partial(shortwave_kernel, slots, first, fresh),
         grid=((end - begin) // SUN_ROWS,),
         out_shape=(
             jax.ShapeDtypeStruct(layer_depth.shape, jnp.float32),
-            jax.ShapeDtypeStruct((1, LANES), jnp.float32),
+            jax.ShapeDtypeStruct((parts, LANES), jnp.float32),
         ),
         in_specs=in_specs,
         out_specs=(cube, line),
@@ -469,7 +534,7 @@
         input_output_aliases=aliases,
         compiler_params=params(),
         cost_estimate=pl.CostEstimate(
-            flops=4 * size, bytes_accessed=8 * size // absorption.shape[0], transcendentals=size
+            flops=4 * size, bytes_accessed=8 * size // absorption.shape[1], transcendentals=size
         ),
         name="shortwave",
     )(*operands)
@@ -526,19 +591,23 @@
     south = lax.ppermute(head, "lat", [(i + 1, i) for i in range(lat_parts - 1)])
 
     half = band_rows // 2
-    sun_args = (absorption, solar, layer_depth, cos_zenith, sunlit, owner_index, slot_index)
-    heating, sent = shortwave(slots, 0, half, *sun_args, jnp.zeros((1, LANES), jnp.float32), None)
+    by_row = (x.reshape(1, band_rows) for x in (sunlit, owner_index, slot_index))
+    sun_args = (absorption.T, solar, layer_depth, cos_zenith, *by_row)
+    heating, sent = shortwave(slots, 0, half, *sun_args, None, None)
+    north, south, sent = lax.optimization_barrier((north, south, sent))
 
     own_west, own_east = edge_columns(depth, mom, north, south, layers)
     west = lax.ppermute(own_east, "lon", [(i, (i + 1) % lon_parts) for i in range(lon_parts)])
     east = lax.ppermute(own_west, "lon", [((i + 1) % lon_parts, i) for i in range(lon_parts)])
 
     heating, sent = shortwave(slots, half, band_rows, *sun_args, sent, heating)
-    arrived = lax.all_gather(sent, "lon", axis=0, tiled=True)
+    arrived = lax.all_to_all(sent, "lon", split_axis=0, concat_axis=0, tiled=True)
+    west, east, sent = lax.optimization_barrier((west, east, sent))
 
     depth_new, mom_new = dynamics(
         gravity, table, depth, mom, north, south, west, east, own_west, own_east
     )
+    arrived, depth_new = lax.optimization_barrier((arrived, depth_new))
     ledger = ledger_of(slots, band_rows // 2, received_counts[0], arrived)
     return (
         depth_new.reshape(layer_depth.shape),

time: 77.4 us -> 54.8 us (0.71)
  the two profiles are of different devices: /device:TPU:2 before, /device:TPU:1 now
where the time goes in v2:
time: 54.8 us; the launch traced here: 54.4 us
  Pallas kernels  38.6 us (70%)
  starting transfers between devices  14.2 us (26%)
  between operations  0.82 us (1%)
  local copies, waits for them, and re-layouts  0.76 us (1%)
    pallas_call x1, Pallas kernels, dynamics(): pl.pallas_call(functools.partial(dynamics_kernel, band_rows), grid=(layer...  19.3 us
    pallas_call x2, Pallas kernels, shortwave(): pl.pallas_call(functools.partial(shortwave_kernel, slots, first, fresh),...  13.5 us
    ppermute x1, starting transfers between devices, body(): lax.ppermute(tail, 'lat', [(i, i + 1) for i in range(lat_parts - 1)])  4.5 us
    all_to_all x1, starting transfers between devices, body(): lax.all_to_all(sent, 'lon', split_axis=0, concat_axis=0, tiled=True)  3.45 us
    ppermute x1, starting transfers between devices, body(): lax.ppermute(own_west, 'lon', [((i + 1) % lon_parts, i) for i in range(lo...  3.1 us
    pallas_call x1, Pallas kernels, edge_columns(): pl.pallas_call(functools.partial(columns_kernel, band_rows), grid=(layers...  2.71 us
    pallas_call x1, Pallas kernels, edge_rows(): pl.pallas_call(kernel, grid=(1,), out_shape=(out, out), in_specs=[pl.Bloc...  1.95 us
    ppermute x1, starting transfers between devices, body(): lax.ppermute(head, 'lat', [(i + 1, i) for i in range(lat_parts - 1)])  1.92 us
  transfers between devices with their start and end apart: 5, of which 0 were waited for; matrix products, arithmetic and copies ran while one was open for 0% of the time, Pallas kernels for 60%

profile of v2, /device:TPU:1, one launch (start us, length us, event | category | flops | bytes accessed | tf_op | source)
XLA Modules:
  0.0 54.4 jit_solution(10450985637366768350)
XLA Ops:
  0.6 0.0 copy-start.1
  0.6 0.0 copy-start.3
  0.7 0.0 copy-start.8
  0.7 0.0 copy-start.7
  0.7 2.0 %edge_rows.1 = (f32[3,2,32,128]{3,2,1,0:T(8,128)}, f32[3,2,32,128]{3,2,1,0:T(8,128)}) custom-call(f32[32,64,128]{2,1,0:T(8,128)} %depth_ref.3, f32[32,64,128]{2,1,0:T(8,128)} %depth_ref.3, f32[2,32,64,128]{3,2,1,0:T(8,128)} %mom_tail.1, f32[2,32,64,128]{3,2,1,0:T(8,128)} %mom_tail.1), custom_call_target="tpu_custom_call" | custom-call | bytes 1048576 | tf_op jit(solution)/shard_map/edge_rows/pallas_call | solution.py:374
  2.7 4.5 %collective-permute-start = (f32[3,2,32,128]{3,2,1,0:T(8,128)}, f32[3,2,32,128]{3,2,1,0:T(8,128)S(1)}, u32[]{:S(2)}, u32[]{:S(2)}) collective-permute-start(f32[3,2,32,128]{3,2,1,0:T(8,128)} %get-tuple-element.22), channel_id=1, source_target_pairs={{0,1},{1,2},{2,3},{4,5},{5,6},{6,7},{8,9},{9,10},{10,11},{12,13},{... | collective-permute-start | bytes 294920 | tf_op jit(solution)/shard_map/ppermute | solution.py:590
  7.2 1.9 %collective-permute-start.1 = (f32[3,2,32,128]{3,2,1,0:T(8,128)}, f32[3,2,32,128]{3,2,1,0:T(8,128)S(1)}, u32[]{:S(2)}, u32[]{:S(2)}) collective-permute-start(f32[3,2,32,128]{3,2,1,0:T(8,128)} %get-tuple-element.23), channel_id=1, source_target_pairs={{1,0},{2,1},{3,2},{5,4},{6,5},{7,6},{9,8},{10,9},{11,10},{13,12},{... | collective-permute-start | bytes 294920 | tf_op jit(solution)/shard_map/ppermute | solution.py:591
  9.2 0.0 copy-start
  9.2 6.8 %shortwave.2 = (f32[32,64,128]{2,1,0:T(8,128)}, f32[8,128]{1,0:T(8,128)S(1)}) custom-call(f32[32,56]{1,0:T(8,128)S(1)} %bitcast.21, f32[1,56]{1,0:T(1,128)S(1)} %bitcast.23, f32[32,64,128]{2,1,0:T(8,128)S(1)} %copy-done.1, f32[64,128]{1,0:T(8,128)S(1)} %copy-done.3, s32[1,64]{1,0:T(1,128)S(1)} %bitcast.25, s32[1,64]{1,0:T(1,128)S(1)} %bitcast.27, ...), custom_call_target="tpu_custom_call" | custom-call | flops 29360128 | bytes 1048576 | tf_op jit(solution)/shard_map/shortwave/pallas_call | solution.py:524
  15.9 0.0 collective-permute-done.north_ref
  15.9 0.0 collective-permute-done.1.south_ref
  16.0 2.7 %edge_columns.1 = (f32[3,2,32,128]{3,2,1,0:T(8,128)S(1)}, f32[3,2,32,128]{3,2,1,0:T(8,128)S(1)}) custom-call(f32[2048,128]{1,0:T(8,128)S(1)} %bitcast.17, f32[2,2048,128]{2,1,0:T(8,128)S(1)} %bitcast.15, f32[3,2,32,128]{3,2,1,0:T(8,128)S(1)} %collective-permute-done.north_ref, f32[3,2,32,128]{3,2,1,0:T(8,128)S(1)} %collective-permute-done.1.south_ref), custom_call_target="tpu_custom_call" | custom-call | flops 3145728 | bytes 3145728 | tf_op jit(solution)/shard_map/edge_columns/pallas_call | solution.py:419
  18.7 1.3 %collective-permute-start.2 = (f32[3,2,32,128]{3,2,1,0:T(8,128)S(1)}, f32[3,2,32,128]{3,2,1,0:T(8,128)}, u32[]{:S(2)}, u32[]{:S(2)}) collective-permute-start(f32[3,2,32,128]{3,2,1,0:T(8,128)S(1)} %get-tuple-element.29.own_east_ref), channel_id=1, source_target_pairs={{0,4},{4,8},{8,12},{12,16},{16,20},{20,24},{24,28},{28,0},{1,5},{5... | collective-permute-start | bytes 294920 | tf_op jit(solution)/shard_map/ppermute | solution.py:600
  19.9 3.1 %collective-permute-start.3 = (f32[3,2,32,128]{3,2,1,0:T(8,128)S(1)}, f32[3,2,32,128]{3,2,1,0:T(8,128)}, u32[]{:S(2)}, u32[]{:S(2)}) collective-permute-start(f32[3,2,32,128]{3,2,1,0:T(8,128)S(1)} %get-tuple-element.30.own_west_ref), channel_id=1, source_target_pairs={{4,0},{8,4},{12,8},{16,12},{20,16},{24,20},{28,24},{0,28},{5,1},{9... | collective-permute-start | bytes 294920 | tf_op jit(solution)/shard_map/ppermute | solution.py:601
  23.0 6.8 %shortwave.3 = (f32[32,64,128]{2,1,0:T(8,128)}, f32[8,128]{1,0:T(8,128)}) custom-call(f32[32,56]{1,0:T(8,128)S(1)} %bitcast.22, f32[1,56]{1,0:T(1,128)S(1)} %bitcast.24, f32[32,64,128]{2,1,0:T(8,128)S(1)} %copy-done.1, f32[64,128]{1,0:T(8,128)S(1)} %copy-done.3, s32[1,64]{1,0:T(1,128)S(1)} %bitcast.26, ...), custom_call_target="tpu_custom_call", output_to_operand_aliasing={{0}: (7, {})} | custom-call | flops 29360128 | bytes 1048576 | tf_op jit(solution)/shard_map/shortwave/pallas_call | solution.py:524
  29.8 3.5 %all-to-all-start = ((f32[8,1,128]{2,1,0:T(1,128)}), f32[8,1,128]{2,1,0:T(1,128)S(1)}, u32[]{:S(2)}, u32[]{:S(2)}) async-start(f32[8,1,128]{2,1,0:T(1,128)} %bitcast.6), calls=%async_computation | async-start | bytes 8192 | tf_op jit(solution)/shard_map/all_to_all | solution.py:604
  33.3 0.0 collective-permute-done.2.west_ref
  33.3 0.0 collective-permute-done.3.east_ref
  33.3 0.0 copy-start.10
  33.3 0.7 %copy-done.10 = f32[32,128]{1,0:T(8,128)S(1)} copy-done((f32[32,128]{1,0:T(8,128)S(1)}, f32[32,128]{1,0:T(8,128)}, u32[]{:S(2)}) %copy-start.10) | copy-done | bytes 16408
  34.0 19.3 %dynamics.1 = (f32[2048,128]{1,0:T(8,128)}, f32[2,2048,128]{2,1,0:T(8,128)}) custom-call(f32[32]{0:T(128)S(1)} %copy-done.9, f32[32,128]{1,0:T(8,128)S(1)} %copy-done.10, f32[32,128]{1,0:T(8,128)S(1)} %copy-done.10, f32[2048,128]{1,0:T(8,128)S(1)} %bitcast.18, f32[2,2048,128]{2,1,0:T(8,128)S(1)} %bitcast.16, ...), custom_call_target="tpu_custom_call" | custom-call | flops 57671680 | bytes 6291456 | tf_op jit(solution)/shard_map/dynamics/pallas_call | solution.py:325
  53.3 0.0 all-to-all-done
  53.3 0.0 copy-done.2
  53.3 1.1 %ledger.1 = f32[1,32]{1,0:T(1,128)} custom-call(s32[1,8]{1,0:T(1,128)S(1)} %bitcast.20, f32[8,128]{1,0:T(8,128)S(1)} %bitcast.19), custom_call_target="tpu_custom_call" | custom-call | tf_op jit(solution)/shard_map/ledger/pallas_call | solution.py:559
  (14 shorter events, 0.0 us)
Async XLA Ops:
  0.6 8.5 %copy-start.1 = (f32[32,64,128]{2,1,0:T(8,128)S(1)}, f32[32,64,128]{2,1,0:T(8,128)}, u32[]{:S(2)}) copy-start(f32[32,64,128]{2,1,0:T(8,128)} %depth_ref.3) | copy-start | bytes 3145732
  0.6 8.5 %copy-start.3 = (f32[64,128]{1,0:T(8,128)S(1)}, f32[64,128]{1,0:T(8,128)}, u32[]{:S(2)}) copy-start(f32[64,128]{1,0:T(8,128)} %sun_ref.3) | copy-start | bytes 98308
  0.7 8.5 %copy-start.8 = (s32[64,1]{0,1:T(1,128)S(1)}, s32[64,1]{0,1:T(1,128)}, u32[]{:S(2)}) copy-start(s32[64,1]{0,1:T(1,128)} %param.19) | copy-start | bytes 772
  0.7 8.5 %copy-start.7 = (s32[64,1]{0,1:T(1,128)S(1)}, s32[64,1]{0,1:T(1,128)}, u32[]{:S(2)}) copy-start(s32[64,1]{0,1:T(1,128)} %param.18) | copy-start | bytes 772
  0.7 8.5 %copy-start.6 = (s32[64,1]{0,1:T(1,128)S(1)}, s32[64,1]{0,1:T(1,128)}, u32[]{:S(2)}) copy-start(s32[64,1]{0,1:T(1,128)} %param.17) | copy-start | bytes 772
  0.7 8.5 %copy-start.5 = (f32[56]{0:T(128)S(1)}, f32[56]{0:T(128)}, u32[]{:S(2)}) copy-start(f32[56]{0:T(128)} %param.15) | copy-start | bytes 676
  0.7 8.5 %copy-start.4 = (f32[56,32]{0,1:T(8,128)S(1)}, f32[56,32]{0,1:T(8,128)}, u32[]{:S(2)}) copy-start(f32[56,32]{0,1:T(8,128)} %param.14) | copy-start | bytes 21508
  2.7 13.3 %collective-permute-start = (f32[3,2,32,128]{3,2,1,0:T(8,128)}, f32[3,2,32,128]{3,2,1,0:T(8,128)S(1)}, u32[]{:S(2)}, u32[]{:S(2)}) collective-permute-start(f32[3,2,32,128]{3,2,1,0:T(8,128)} %get-tuple-element.22), channel_id=1, source_target_pairs={{0,1},{1,2},{2,3},{4,5},{5,6},{6,7},{8,9},{9,10},{10,11},{12,13},{... | collective-permute-start | bytes 294920 | tf_op jit(solution)/shard_map/ppermute | solution.py:590
  7.2 8.8 %collective-permute-start.1 = (f32[3,2,32,128]{3,2,1,0:T(8,128)}, f32[3,2,32,128]{3,2,1,0:T(8,128)S(1)}, u32[]{:S(2)}, u32[]{:S(2)}) collective-permute-start(f32[3,2,32,128]{3,2,1,0:T(8,128)} %get-tuple-element.23), channel_id=1, source_target_pairs={{1,0},{2,1},{3,2},{5,4},{6,5},{7,6},{9,8},{10,9},{11,10},{13,12},{... | collective-permute-start | bytes 294920 | tf_op jit(solution)/shard_map/ppermute | solution.py:591
  9.2 6.8 %copy-start = (f32[2,32,64,128]{3,2,1,0:T(8,128)S(1)}, f32[2,32,64,128]{3,2,1,0:T(8,128)}, u32[]{:S(2)}) copy-start(f32[2,32,64,128]{3,2,1,0:T(8,128)} %mom_tail.1) | copy-start | bytes 6291460
  18.7 14.6 %collective-permute-start.2 = (f32[3,2,32,128]{3,2,1,0:T(8,128)S(1)}, f32[3,2,32,128]{3,2,1,0:T(8,128)}, u32[]{:S(2)}, u32[]{:S(2)}) collective-permute-start(f32[3,2,32,128]{3,2,1,0:T(8,128)S(1)} %get-tuple-element.29.own_east_ref), channel_id=1, source_target_pairs={{0,4},{4,8},{8,12},{12,16},{16,20},{20,24},{24,28},{28,0},{1,5},{5... | collective-permute-start | bytes 294920 | tf_op jit(solution)/shard_map/ppermute | solution.py:600
  19.9 13.4 %collective-permute-start.3 = (f32[3,2,32,128]{3,2,1,0:T(8,128)S(1)}, f32[3,2,32,128]{3,2,1,0:T(8,128)}, u32[]{:S(2)}, u32[]{:S(2)}) collective-permute-start(f32[3,2,32,128]{3,2,1,0:T(8,128)S(1)} %get-tuple-element.30.own_west_ref), channel_id=1, source_target_pairs={{4,0},{8,4},{12,8},{16,12},{20,16},{24,20},{28,24},{0,28},{5,1},{9... | collective-permute-start | bytes 294920 | tf_op jit(solution)/shard_map/ppermute | solution.py:601
  23.0 10.3 %copy-start.9 = (f32[32]{0:T(128)S(1)}, f32[32]{0:T(128)}, u32[]{:S(2)}) copy-start(f32[32]{0:T(128)} %gravity_ref.1) | copy-start | bytes 388
  29.8 23.5 %copy-start.2 = (s32[1,1,8]{2,1,0:T(1,128)S(1)}, s32[1,1,8]{2,1,0:T(1,128)}, u32[]{:S(2)}) copy-start(s32[1,1,8]{2,1,0:T(1,128)} %param.20) | copy-start | bytes 100
  29.8 23.5 %all-to-all-start = ((f32[8,1,128]{2,1,0:T(1,128)}), f32[8,1,128]{2,1,0:T(1,128)S(1)}, u32[]{:S(2)}, u32[]{:S(2)}) async-start(f32[8,1,128]{2,1,0:T(1,128)} %bitcast.6), calls=%async_computation | async-start | bytes 8192 | tf_op jit(solution)/shard_map/all_to_all | solution.py:604
  33.3 0.7 %copy-start.10 = (f32[32,128]{1,0:T(8,128)S(1)}, f32[32,128]{1,0:T(8,128)}, u32[]{:S(2)}) copy-start(f32[32,128]{1,0:T(8,128)} %constant.2.clone.table_ref.lanes_ref) | copy-start | bytes 49156
